TPU v7x, 128 devices: a whole 4x4x4 slice. The times are simulated.
128 devices in a mesh: leaf: 128 (over x, z, y, core).
Axes of the slice: x: 4, y: 4, z: 4, core: 2. Of those that a mesh axis runs over, the one named last changes fastest.
Arguments:
- coords: float32 [2048, 3, 512], P('leaf'), may hold values from 0 to 1
- charges: float32 [2048, 4, 512], P('leaf'), may hold values from -6 to 6
- bases: float32 [2048, 64, 512], P('leaf'), may hold values from -0.25 to 0.25
- up_transfer: float32 [2048, 64, 64], P('leaf'), may hold values from -0.25 to 0.25
- top_transfer: float32 [256, 64, 64], P('leaf'), may hold values from -0.75 to 0.75
- proxy_mid: float32 [256, 3, 64], replicated, may hold values from 0 to 1
- proxy_top: float32 [32, 3, 64], replicated, may hold values from 0 to 1
- near_list: int32 [2048, 4], P('leaf'), may hold values from 0 to 2047, as said below
- near_count: int32 [2048], P('leaf'), may hold values from 1 to 4
- far_mid: int32 [256, 32], replicated, may hold values from 0 to 255, as said below
- far_mid_count: int32 [256], replicated, may hold values from 16 to 32
- far_top: int32 [32, 6], replicated, may hold values from 0 to 31, as said below
- far_top_count: int32 [32], replicated, may hold values from 1 to 6
Outputs:
- field: float32 [2048, 4, 512], P('leaf')
Inputs may be any that keep to these rules, and one draw needn't show every extreme that they name: `near_list`: slot 0 of leaf l's list is l itself; the slots of a list are distinct; with 16 leaves a device in Morton order, every entry of a leaf held by device d names a leaf of device d, one of the last 8 leaves of device d - 1 or one of the first 8 leaves of device d + 1. `far_mid`: the slots of a row are distinct nodes other than the row's own node. `far_top`: the slots of a row are distinct nodes other than the row's own node.
All inputs are finite; a program needn't handle non-finite values.
Results may differ from a plain program's by a relative error of at most 0.0003.
Values sent between devices are 32-bit elements; how exact they have to be, the bound alone decides.
No kernel may reach another device: no remote copies, remote signals or barrier semaphores. Data moves between devices by JAX's collectives and lax.ppermute only.
A program may use at most 64 MiB of HBM per device.

v0:
```python
import jax
import jax.numpy as jnp
from jax import lax
from jax.sharding import PartitionSpec as P

EDGE = 8


length_scale = 0.4
out_scale = 0.125
precise = lax.Precision.HIGHEST


def extended(value, sides, width):
    for axis, dim in sides:
        peers, length = (lax.axis_size(axis), value.shape[dim])
        up = [(i, (i + 1) % peers) for i in range(peers - 1)]
        down = [(j, i) for i, j in up]
        last = lax.slice_in_dim(value, length - width, length, axis=dim)
        first = lax.slice_in_dim(value, 0, width, axis=dim)
        before = lax.ppermute(last, axis, up)
        after = lax.ppermute(first, axis, down)
        value = jnp.concatenate([before, value, after], axis=dim)
    return value


def side_by_side(arrays, axis, dim, along):
    both = jnp.concatenate(arrays, axis=along)
    filled, at, outs = (lax.all_gather(both, axis, axis=dim, tiled=True), 0, [])
    for a in arrays:
        outs.append(lax.slice_in_dim(filled, at, at + a.shape[along], axis=along))
        at += a.shape[along]
    return tuple(outs)


def kernel(target_pts, source_pts):
    offset = target_pts[:, :, None] - source_pts[:, None, :]
    return jnp.exp(-jnp.sqrt(jnp.sum(offset * offset, axis=0)) / length_scale)


def couple(target_proxy, source_proxy, coeffs, source_lists, counts):

    def single_target(packed_args):
        target_pts, source_ids, live_count = packed_args
        kernels = jax.vmap(kernel, (None, 0))(target_pts, source_proxy[source_ids])
        live_mask = (jnp.arange(source_ids.shape[0]) < live_count).astype(jnp.float32)
        return jnp.einsum(
            "jab,jbk->ak", kernels * live_mask[:, None, None], coeffs[source_ids], precision=precise
        )

    return lax.map(single_target, (target_proxy, source_lists, counts))


def shards(
    coords,
    charges,
    bases,
    up_transfer,
    top_transfer,
    proxy_mid,
    proxy_top,
    near_list,
    near_count,
    far_mid,
    far_mid_count,
    far_top,
    far_top_count,
):
    leaves = coords.shape[0]
    mid_nodes = leaves // 8
    ranks = bases.shape[1]
    vectors = charges.shape[1]
    device = lax.axis_index("leaf")
    packed = jnp.concatenate([coords, charges], axis=1)
    window = extended(packed, (("leaf", 0),), EDGE)
    window_start = device * leaves - EDGE

    def near_leaf(packed_args):
        target_pts, source_ids, live_count = packed_args
        source_rows = jnp.take(window, source_ids - window_start, axis=0)
        blocks = jax.vmap(kernel, (None, 0))(target_pts, source_rows[:, :3])
        live_mask = (jnp.arange(source_ids.shape[0]) < live_count).astype(jnp.float32)
        source_vals = source_rows[:, 3:] * live_mask[:, None, None]
        return jnp.einsum("jts,jks->kt", blocks, source_vals, precision=precise)

    near_part = lax.map(near_leaf, (coords, near_list, near_count))
    leaf_coeffs = jnp.einsum("lrp,lkp->lrk", bases, charges, precision=precise)
    lifted_leaf = jnp.einsum("lrs,lsk->lrk", up_transfer, leaf_coeffs, precision=precise)
    mid_coeffs = lifted_leaf.reshape(mid_nodes, 8, ranks, vectors).sum(1)
    lifted_mid = jnp.einsum("nrs,nsk->nrk", top_transfer, mid_coeffs, precision=precise)
    mid_start = device * mid_nodes
    own_ids = mid_start + jnp.arange(mid_nodes)
    own_proxy = lax.dynamic_slice_in_dim(proxy_mid, mid_start, mid_nodes, 0)
    parents = own_ids // 8
    every_mid, every_lift = side_by_side((mid_coeffs, lifted_mid), "leaf", 0, 1)
    top_coeffs = every_lift.reshape(-1, 8, ranks, vectors).sum(1)
    own_lists = lax.dynamic_slice_in_dim(far_mid, mid_start, mid_nodes, 0)
    own_counts = lax.dynamic_slice_in_dim(far_mid_count, mid_start, mid_nodes, 0)
    mid_far = couple(own_proxy, proxy_mid, every_mid, own_lists, own_counts)
    top_field = couple(
        proxy_top[parents], proxy_top, top_coeffs, far_top[parents], far_top_count[parents]
    )
    mid_field = mid_far + jnp.einsum("nsr,nsk->nrk", top_transfer, top_field, precision=precise)
    leaf_field = jnp.einsum(
        "nsr,nsk->nrk", up_transfer, jnp.repeat(mid_field, 8, axis=0), precision=precise
    )
    far_part = jnp.einsum("lrp,lrk->lkp", bases, leaf_field, precision=precise)
    return (near_part + far_part) * out_scale


def solution(mesh):
    placed = (
        P("leaf", None, None),
        P("leaf", None, None),
        P("leaf", None, None),
        P("leaf", None, None),
        P("leaf", None, None),
        P(),
        P(),
        P("leaf", None),
        P("leaf"),
        P(),
        P(),
        P(),
        P(),
    )
    return jax.shard_map(
        shards, mesh=mesh, in_specs=placed, out_specs=P("leaf", None, None), check_vma=False
    )
```

profile of v0, /device:TPU:1, one launch (start us, length us, event | category | flops | bytes accessed | tf_op | source)
XLA Modules:
  0.0 210.0 jit_solution(16865515241557585296)
XLA Ops:
  0.0 1.1 copy.43
  1.1 1.6 fusion.39
  2.7 3.3 %collective-permute-start.1 = (f32[8,7,512]{2,1,0:T(8,128)}, f32[8,7,512]{2,1,0:T(8,128)}, u32[]{:S(2)}, u32[]{:S(2)}) collective-permute-start(f32[8,7,512]{2,1,0:T(8,128)} %get-tuple-element.239), channel_id=1, source_target_pairs={{1,0},{2,1},{3,2},{4,3},{5,4},{6,5},{7,6},{8,7},{9,8},{10,9},{11,1... | collective-permute-start | bytes 344072 | tf_op jit(solution)/shard_map/ppermute | solution.py:22
  6.0 3.2 %collective-permute-start = (f32[8,7,512]{2,1,0:T(8,128)}, f32[8,7,512]{2,1,0:T(8,128)}, u32[]{:S(2)}, u32[]{:S(2)}) collective-permute-start(f32[8,7,512]{2,1,0:T(8,128)} %get-tuple-element.238), channel_id=1, source_target_pairs={{0,1},{1,2},{2,3},{3,4},{4,5},{5,6},{6,7},{7,8},{8,9},{9,10},{10,1... | collective-permute-start | bytes 344072 | tf_op jit(solution)/shard_map/ppermute | solution.py:21
  9.8 1.2 copy.46
  11.0 0.8 constant_dynamic-slice_fusion.4
  11.8 0.7 copy.53
  12.4 1.3 dynamic_slice.45
  13.7 2.8 %fusion.41 = f32[16,64,4]{1,2,0:T(4,128)S(1)} fusion(f32[16,64,512]{2,1,0:T(8,128)S(1)} %copy-done, f32[16,4,512]{2,1,0:T(4,128)} %param.20), kind=kOutput, calls=%fused_computation.88 | convolution fusion | flops 25165824 | bytes 2244608 | tf_op jit(solution)/shard_map/lrp,lkp->lrk/dot_general | solution.py:87
  16.5 2.0 bitcast_reduce_fusion.1
  18.8 40.7 %all_gather.3 = f32[256,128,4]{1,2,0:T(4,128)S(1)} all-gather(f32[2,128,4]{1,2,0:T(4,128)S(1)} %pad_maximum_fusion.2), channel_id=1, replica_groups=mesh['leaf'=128] {'leaf'}, dimensions={0}, use_global_device_ids=true | all-gather | bytes 528384 | tf_op jit(solution)/shard_map/all_gather | solution.py:29
  59.8 11.4 %while.31 = (s32[]{:T(128)}, f32[2,64,4]{1,2,0:T(4,128)S(1)}, f32[2,3,64]{2,1,0:T(4,128)S(1)}, s32[2,32]{1,0:T(2,128)}, f32[256,3,64]{2,1,0:T(4,128)S(1)}, /*ind...) while((s32[]{:T(128)}, f32[2,64,4]{1,2,0:T(4,128)S(1)}, f32[2,3,64]{2,1,0:T(4,128)S(1)}, s32[2,32]{1,0:T(2,128)}, ...), condition=%wide.region_6.7_spmd, body=%wide.region_4.6_spmd.sunk | while | flops 7734434 | bytes 1787513 | solution.py:51
  59.8 0.7 fusion.74
  62.3 1.3 dynamic_slice.88
  64.2 1.3 fusion.75
  65.5 0.7 fusion.74
  68.0 1.3 dynamic_slice.88
  69.9 1.3 fusion.75
  71.2 0.7 pad_clamp_fusion.3
  71.9 0.8 copy.51
  72.7 1.4 gather_fusion.5
  74.1 0.8 copy.49
  76.1 5.9 %while.32 = (s32[]{:T(128)}, f32[2,64,4]{1,2,0:T(4,128)S(1)}, f32[2,3,64]{2,0,1:T(2,128)S(1)}, s32[2,6]{1,0:T(2,128)S(1)}, f32[32,3,64]{2,1,0:T(4,128)S(1)}, /*i...) while((s32[]{:T(128)}, f32[2,64,4]{1,2,0:T(4,128)S(1)}, f32[2,3,64]{2,0,1:T(2,128)S(1)}, ...), condition=%wide.region_10.11_spmd, body=%wide.region_8.10_spmd.sunk | while | flops 1451040 | bytes 344073 | solution.py:51
  77.4 0.7 dynamic_slice.91
  80.4 0.7 dynamic_slice.91
  82.8 1.1 fusion.43
  84.0 1.1 pad_maximum_fusion
  85.1 124.2 %while.30 = (s32[]{:T(128)}, f32[16,4,512]{2,1,0:T(4,128)S(1)}, s32[16,4]{1,0:T(8,128)S(1)}, s32[]{:T(128)}, f32[32,7,512]{2,1,0:T(8,128)S(1)}, /*index=5*/s32[16]{0:T(128)S(1)}, f32[16,3,512]{2,1,0:T(4,128)S(1)}, s32[]{:T(128)}) while((s32[]{:T(128)}, f32[16,4,512]{2,1,0:T(4,128)S(1)}, s32[16,4]{1,0:T(8,128)S(1)}, s32[]{:T(128)}, ...), condition=%wide.region_2.3_spmd, body=%wide.region_0.2_spmd.sunk | while | flops 60841012 | bytes 8755949 | solution.py:86
  85.8 1.3 multiply_reduce_fusion.6
  87.6 0.6 compare_convert_fusion.6
  88.3 4.5 %fusion.71 = f32[16,4,512]{2,1,0:T(4,128)S(1)} fusion(f32[16,4,512]{2,1,0:T(4,128)S(1)} %get-tuple-element.378, s32[]{:T(128)S(6)} %copy.63, f32[4,512,512]{2,1,0:T(8,128)S(1)} %multiply_reduce_fusion.6, f32[4,7,512]{2,1,0:T(8,128)S(1)} %broadcast_select_fusion.2, f32[4]{0:T(128)S(1)} %compare_convert_fusion.6), kind=kOutput, calls=%fused_computation.16.clone.1 | convolution fusion | flops 52436992 | bytes 4235780 | tf_op jit(solution)/shard_map/while/body/eval_jaxpr/jts,jks->kt/dot_general | solution.py:84
  93.6 1.3 multiply_reduce_fusion.6
  95.4 0.6 compare_convert_fusion.6
  96.1 4.5 %fusion.71 = f32[16,4,512]{2,1,0:T(4,128)S(1)} fusion(f32[16,4,512]{2,1,0:T(4,128)S(1)} %get-tuple-element.378, s32[]{:T(128)S(6)} %copy.63, f32[4,512,512]{2,1,0:T(8,128)S(1)} %multiply_reduce_fusion.6, f32[4,7,512]{2,1,0:T(8,128)S(1)} %broadcast_select_fusion.2, f32[4]{0:T(128)S(1)} %compare_convert_fusion.6), kind=kOutput, calls=%fused_computation.16.clone.1 | convolution fusion | flops 52436992 | bytes 4235780 | tf_op jit(solution)/shard_map/while/body/eval_jaxpr/jts,jks->kt/dot_general | solution.py:84
  101.3 1.3 multiply_reduce_fusion.6
  103.8 4.5 %fusion.71 = f32[16,4,512]{2,1,0:T(4,128)S(1)} fusion(f32[16,4,512]{2,1,0:T(4,128)S(1)} %get-tuple-element.378, s32[]{:T(128)S(6)} %copy.63, f32[4,512,512]{2,1,0:T(8,128)S(1)} %multiply_reduce_fusion.6, f32[4,7,512]{2,1,0:T(8,128)S(1)} %broadcast_select_fusion.2, f32[4]{0:T(128)S(1)} %compare_convert_fusion.6), kind=kOutput, calls=%fused_computation.16.clone.1 | convolution fusion | flops 52436992 | bytes 4235780 | tf_op jit(solution)/shard_map/while/body/eval_jaxpr/jts,jks->kt/dot_general | solution.py:84
  109.1 1.3 multiply_reduce_fusion.6
  111.6 4.5 %fusion.71 = f32[16,4,512]{2,1,0:T(4,128)S(1)} fusion(f32[16,4,512]{2,1,0:T(4,128)S(1)} %get-tuple-element.378, s32[]{:T(128)S(6)} %copy.63, f32[4,512,512]{2,1,0:T(8,128)S(1)} %multiply_reduce_fusion.6, f32[4,7,512]{2,1,0:T(8,128)S(1)} %broadcast_select_fusion.2, f32[4]{0:T(128)S(1)} %compare_convert_fusion.6), kind=kOutput, calls=%fused_computation.16.clone.1 | convolution fusion | flops 52436992 | bytes 4235780 | tf_op jit(solution)/shard_map/while/body/eval_jaxpr/jts,jks->kt/dot_general | solution.py:84
  116.8 1.3 multiply_reduce_fusion.6
  119.4 4.5 %fusion.71 = f32[16,4,512]{2,1,0:T(4,128)S(1)} fusion(f32[16,4,512]{2,1,0:T(4,128)S(1)} %get-tuple-element.378, s32[]{:T(128)S(6)} %copy.63, f32[4,512,512]{2,1,0:T(8,128)S(1)} %multiply_reduce_fusion.6, f32[4,7,512]{2,1,0:T(8,128)S(1)} %broadcast_select_fusion.2, f32[4]{0:T(128)S(1)} %compare_convert_fusion.6), kind=kOutput, calls=%fused_computation.16.clone.1 | convolution fusion | flops 52436992 | bytes 4235780 | tf_op jit(solution)/shard_map/while/body/eval_jaxpr/jts,jks->kt/dot_general | solution.py:84
  124.6 1.3 multiply_reduce_fusion.6
  127.1 4.5 %fusion.71 = f32[16,4,512]{2,1,0:T(4,128)S(1)} fusion(f32[16,4,512]{2,1,0:T(4,128)S(1)} %get-tuple-element.378, s32[]{:T(128)S(6)} %copy.63, f32[4,512,512]{2,1,0:T(8,128)S(1)} %multiply_reduce_fusion.6, f32[4,7,512]{2,1,0:T(8,128)S(1)} %broadcast_select_fusion.2, f32[4]{0:T(128)S(1)} %compare_convert_fusion.6), kind=kOutput, calls=%fused_computation.16.clone.1 | convolution fusion | flops 52436992 | bytes 4235780 | tf_op jit(solution)/shard_map/while/body/eval_jaxpr/jts,jks->kt/dot_general | solution.py:84
  132.4 1.3 multiply_reduce_fusion.6
  134.9 4.5 %fusion.71 = f32[16,4,512]{2,1,0:T(4,128)S(1)} fusion(f32[16,4,512]{2,1,0:T(4,128)S(1)} %get-tuple-element.378, s32[]{:T(128)S(6)} %copy.63, f32[4,512,512]{2,1,0:T(8,128)S(1)} %multiply_reduce_fusion.6, f32[4,7,512]{2,1,0:T(8,128)S(1)} %broadcast_select_fusion.2, f32[4]{0:T(128)S(1)} %compare_convert_fusion.6), kind=kOutput, calls=%fused_computation.16.clone.1 | convolution fusion | flops 52436992 | bytes 4235780 | tf_op jit(solution)/shard_map/while/body/eval_jaxpr/jts,jks->kt/dot_general | solution.py:84
  140.1 1.3 multiply_reduce_fusion.6
  142.0 0.6 compare_convert_fusion.6
  142.6 4.5 %fusion.71 = f32[16,4,512]{2,1,0:T(4,128)S(1)} fusion(f32[16,4,512]{2,1,0:T(4,128)S(1)} %get-tuple-element.378, s32[]{:T(128)S(6)} %copy.63, f32[4,512,512]{2,1,0:T(8,128)S(1)} %multiply_reduce_fusion.6, f32[4,7,512]{2,1,0:T(8,128)S(1)} %broadcast_select_fusion.2, f32[4]{0:T(128)S(1)} %compare_convert_fusion.6), kind=kOutput, calls=%fused_computation.16.clone.1 | convolution fusion | flops 52436992 | bytes 4235780 | tf_op jit(solution)/shard_map/while/body/eval_jaxpr/jts,jks->kt/dot_general | solution.py:84
  147.9 1.3 multiply_reduce_fusion.6
  150.4 4.5 %fusion.71 = f32[16,4,512]{2,1,0:T(4,128)S(1)} fusion(f32[16,4,512]{2,1,0:T(4,128)S(1)} %get-tuple-element.378, s32[]{:T(128)S(6)} %copy.63, f32[4,512,512]{2,1,0:T(8,128)S(1)} %multiply_reduce_fusion.6, f32[4,7,512]{2,1,0:T(8,128)S(1)} %broadcast_select_fusion.2, f32[4]{0:T(128)S(1)} %compare_convert_fusion.6), kind=kOutput, calls=%fused_computation.16.clone.1 | convolution fusion | flops 52436992 | bytes 4235780 | tf_op jit(solution)/shard_map/while/body/eval_jaxpr/jts,jks->kt/dot_general | solution.py:84
  155.7 1.3 multiply_reduce_fusion.6
  158.2 4.5 %fusion.71 = f32[16,4,512]{2,1,0:T(4,128)S(1)} fusion(f32[16,4,512]{2,1,0:T(4,128)S(1)} %get-tuple-element.378, s32[]{:T(128)S(6)} %copy.63, f32[4,512,512]{2,1,0:T(8,128)S(1)} %multiply_reduce_fusion.6, f32[4,7,512]{2,1,0:T(8,128)S(1)} %broadcast_select_fusion.2, f32[4]{0:T(128)S(1)} %compare_convert_fusion.6), kind=kOutput, calls=%fused_computation.16.clone.1 | convolution fusion | flops 52436992 | bytes 4235780 | tf_op jit(solution)/shard_map/while/body/eval_jaxpr/jts,jks->kt/dot_general | solution.py:84
  163.4 1.3 multiply_reduce_fusion.6
  165.9 4.5 %fusion.71 = f32[16,4,512]{2,1,0:T(4,128)S(1)} fusion(f32[16,4,512]{2,1,0:T(4,128)S(1)} %get-tuple-element.378, s32[]{:T(128)S(6)} %copy.63, f32[4,512,512]{2,1,0:T(8,128)S(1)} %multiply_reduce_fusion.6, f32[4,7,512]{2,1,0:T(8,128)S(1)} %broadcast_select_fusion.2, f32[4]{0:T(128)S(1)} %compare_convert_fusion.6), kind=kOutput, calls=%fused_computation.16.clone.1 | convolution fusion | flops 52436992 | bytes 4235780 | tf_op jit(solution)/shard_map/while/body/eval_jaxpr/jts,jks->kt/dot_general | solution.py:84
  171.2 1.3 multiply_reduce_fusion.6
  173.7 4.5 %fusion.71 = f32[16,4,512]{2,1,0:T(4,128)S(1)} fusion(f32[16,4,512]{2,1,0:T(4,128)S(1)} %get-tuple-element.378, s32[]{:T(128)S(6)} %copy.63, f32[4,512,512]{2,1,0:T(8,128)S(1)} %multiply_reduce_fusion.6, f32[4,7,512]{2,1,0:T(8,128)S(1)} %broadcast_select_fusion.2, f32[4]{0:T(128)S(1)} %compare_convert_fusion.6), kind=kOutput, calls=%fused_computation.16.clone.1 | convolution fusion | flops 52436992 | bytes 4235780 | tf_op jit(solution)/shard_map/while/body/eval_jaxpr/jts,jks->kt/dot_general | solution.py:84
  178.9 1.3 multiply_reduce_fusion.6
  181.5 4.5 %fusion.71 = f32[16,4,512]{2,1,0:T(4,128)S(1)} fusion(f32[16,4,512]{2,1,0:T(4,128)S(1)} %get-tuple-element.378, s32[]{:T(128)S(6)} %copy.63, f32[4,512,512]{2,1,0:T(8,128)S(1)} %multiply_reduce_fusion.6, f32[4,7,512]{2,1,0:T(8,128)S(1)} %broadcast_select_fusion.2, f32[4]{0:T(128)S(1)} %compare_convert_fusion.6), kind=kOutput, calls=%fused_computation.16.clone.1 | convolution fusion | flops 52436992 | bytes 4235780 | tf_op jit(solution)/shard_map/while/body/eval_jaxpr/jts,jks->kt/dot_general | solution.py:84
  186.7 1.3 multiply_reduce_fusion.6
  189.2 4.5 %fusion.71 = f32[16,4,512]{2,1,0:T(4,128)S(1)} fusion(f32[16,4,512]{2,1,0:T(4,128)S(1)} %get-tuple-element.378, s32[]{:T(128)S(6)} %copy.63, f32[4,512,512]{2,1,0:T(8,128)S(1)} %multiply_reduce_fusion.6, f32[4,7,512]{2,1,0:T(8,128)S(1)} %broadcast_select_fusion.2, f32[4]{0:T(128)S(1)} %compare_convert_fusion.6), kind=kOutput, calls=%fused_computation.16.clone.1 | convolution fusion | flops 52436992 | bytes 4235780 | tf_op jit(solution)/shard_map/while/body/eval_jaxpr/jts,jks->kt/dot_general | solution.py:84
  194.5 1.3 multiply_reduce_fusion.6
  197.0 4.5 %fusion.71 = f32[16,4,512]{2,1,0:T(4,128)S(1)} fusion(f32[16,4,512]{2,1,0:T(4,128)S(1)} %get-tuple-element.378, s32[]{:T(128)S(6)} %copy.63, f32[4,512,512]{2,1,0:T(8,128)S(1)} %multiply_reduce_fusion.6, f32[4,7,512]{2,1,0:T(8,128)S(1)} %broadcast_select_fusion.2, f32[4]{0:T(128)S(1)} %compare_convert_fusion.6), kind=kOutput, calls=%fused_computation.16.clone.1 | convolution fusion | flops 52436992 | bytes 4235780 | tf_op jit(solution)/shard_map/while/body/eval_jaxpr/jts,jks->kt/dot_general | solution.py:84
  202.2 1.3 multiply_reduce_fusion.6
  204.7 4.5 %fusion.71 = f32[16,4,512]{2,1,0:T(4,128)S(1)} fusion(f32[16,4,512]{2,1,0:T(4,128)S(1)} %get-tuple-element.378, s32[]{:T(128)S(6)} %copy.63, f32[4,512,512]{2,1,0:T(8,128)S(1)} %multiply_reduce_fusion.6, f32[4,7,512]{2,1,0:T(8,128)S(1)} %broadcast_select_fusion.2, f32[4]{0:T(128)S(1)} %compare_convert_fusion.6), kind=kOutput, calls=%fused_computation.16.clone.1 | convolution fusion | flops 52436992 | bytes 4235780 | tf_op jit(solution)/shard_map/while/body/eval_jaxpr/jts,jks->kt/dot_general | solution.py:84
  209.3 0.7 add_multiply_fusion
  (201 shorter events, 41.5 us)
Async XLA Ops:
  0.0 13.7 %copy-start = (f32[16,64,512]{2,1,0:T(8,128)S(1)}, f32[16,64,512]{2,1,0:T(8,128)}, u32[]{:S(2)}) copy-start(f32[16,64,512]{2,1,0:T(8,128)} %param.21) | copy-start | bytes 6291460
  0.0 18.5 %copy-start.4 = (f32[2,64,64]{2,1,0:T(8,128)S(1)}, f32[2,64,64]{2,1,0:T(8,128)}, u32[]{:S(2)}) copy-start(f32[2,64,64]{2,1,0:T(8,128)} %param.23) | copy-start | bytes 98308
  2.7 81.2 %collective-permute-start.1 = (f32[8,7,512]{2,1,0:T(8,128)}, f32[8,7,512]{2,1,0:T(8,128)}, u32[]{:S(2)}, u32[]{:S(2)}) collective-permute-start(f32[8,7,512]{2,1,0:T(8,128)} %get-tuple-element.239), channel_id=1, source_target_pairs={{1,0},{2,1},{3,2},{4,3},{5,4},{6,5},{7,6},{8,7},{9,8},{10,9},{11,1... | collective-permute-start | bytes 344072 | tf_op jit(solution)/shard_map/ppermute | solution.py:22
  6.0 78.0 %collective-permute-start = (f32[8,7,512]{2,1,0:T(8,128)}, f32[8,7,512]{2,1,0:T(8,128)}, u32[]{:S(2)}, u32[]{:S(2)}) collective-permute-start(f32[8,7,512]{2,1,0:T(8,128)} %get-tuple-element.238), channel_id=1, source_target_pairs={{0,1},{1,2},{2,3},{3,4},{4,5},{5,6},{6,7},{7,8},{8,9},{9,10},{10,1... | collective-permute-start | bytes 344072 | tf_op jit(solution)/shard_map/ppermute | solution.py:21
  59.8 15.6 %copy-start.1 = (s32[32]{0:T(128)S(1)}, s32[32]{0:T(128)}, u32[]{:S(2)}) copy-start(s32[32]{0:T(128)} %param.31) | copy-start | bytes 388
  71.2 11.0 %copy-start.2 = (f32[16,64,64]{2,1,0:T(8,128)S(1)}, f32[16,64,64]{2,1,0:T(8,128)}, u32[]{:S(2)}) copy-start(f32[16,64,64]{2,1,0:T(8,128)} %param.22) | copy-start | bytes 786436
  71.2 12.7 %copy-start.5 = (s32[16,4]{0,1:T(4,128)S(1)}, s32[16,4]{0,1:T(4,128)}, u32[]{:S(2)}) copy-start(s32[16,4]{0,1:T(4,128)} %param.26) | copy-start | bytes 772
  71.2 12.8 %copy-start.3 = (f32[16,4,512]{2,1,0:T(4,128)S(1)}, f32[16,4,512]{2,1,0:T(4,128)}, u32[]{:S(2)}) copy-start(f32[16,4,512]{2,1,0:T(4,128)} %param.20) | copy-start | bytes 393220
  76.1 9.0 %copy-start.6 = (s32[16]{0:T(128)S(1)}, s32[16]{0:T(128)}, u32[]{:S(2)}) copy-start(s32[16]{0:T(128)} %param.27) | copy-start | bytes 196
where the time goes:
time: 211 us; the launch traced here: 210 us
  matrix products  82.4 us (39%)
  other arithmetic  42.7 us (20%)
  blocking collectives  40.7 us (19%)
  local copies, waits for them, and re-layouts  36.5 us (17%)
  starting transfers between devices  6.49 us (3%)
    dot_general x16, matrix products, near_leaf(): return jnp.einsum('jts,jks->kt', blocks, source_vals, precision=precise)  72.4 us
    all_gather x1, blocking collectives, side_by_side(): filled, at, outs = (lax.all_gather(both, axis, axis=dim, tiled=True), 0, [])  40.7 us
    reduce_sum x20, other arithmetic, kernel(): return jnp.exp(-jnp.sqrt(jnp.sum(offset * offset, axis=0)) / length_scale)  21.4 us
    convert_element_type x16, other arithmetic, near_leaf(): (jnp.arange(source_ids.shape[0]) < live_count).astype(jnp.float32)  10.3 us
    dynamic_slice x16, local copies, waits for them, and re-layouts, shards(): near_part = lax.map(near_leaf, (coords, near_list, near_count))  9.42 us
    gather x16, local copies, waits for them, and re-layouts, near_leaf(): source_rows = jnp.take(window, source_ids - window_start, axis=0)  8.84 us
  transfers between devices with their start and end apart: 2, of which 0 were waited for; matrix products, arithmetic and copies ran while one was open for 16% of the time, Pallas kernels for 0%

commit v1 on v0

v1 whole, which is shorter than its diff:
```python
import functools

import jax
import jax.numpy as jnp
from jax import lax
from jax.experimental import pallas as pl
from jax.experimental.pallas import tpu as pltpu
from jax.sharding import PartitionSpec as P

EDGE = 8
NRHS = 4
length_scale = 0.4
out_scale = 0.125
TINY = 1e-30
RATE = -1.4426950408889634 / length_scale
NT = (((1,), (1,)), ((), ()))
TN = (((0,), (0,)), ((), ()))
bf16 = jnp.bfloat16
f32 = jnp.float32
VM = pl.BlockSpec(memory_space=pltpu.VMEM)
SM = pl.BlockSpec(memory_space=pltpu.SMEM)
ANY = pl.BlockSpec(memory_space=pl.ANY)
VMEM_LIMIT = 56 * 2**20


def snap(value, magic):
    return (value + magic) - magic


def split2(value):
    high = value.astype(bf16)
    return high, (value - high.astype(f32)).astype(bf16)


def rows8(value):
    high, low = split2(value)
    return jnp.concatenate([high.astype(f32), low.astype(f32)], axis=0).astype(bf16)


def fold8(value):
    return value[0:NRHS] + value[NRHS : 2 * NRHS]


def dot2(rows, value, dims):
    high, low = split2(value)
    return lax.dot_general(rows, high, dims, preferred_element_type=f32) + lax.dot_general(
        rows, low, dims, preferred_element_type=f32
    )


def features(points):
    x = points - 0.5
    h = snap(x, 49152.0)
    low = x - h
    l0 = snap(low, 96.0)
    l1 = low - l0
    n = jnp.sum(h * h, axis=0, keepdims=True)
    n0 = snap(n, 49152.0)
    n1 = n - n0
    m = jnp.sum(low * (h + h + low), axis=0, keepdims=True)
    m0 = snap(m, 384.0)
    rest = m - m0
    m1 = snap(rest, 1.5)
    m2 = rest - m1
    one = jnp.ones_like(n0)
    return jnp.concatenate([h, n0, n1, one, one, m0, l0, l1, m1, m2], axis=0).astype(bf16)


def mixing():
    r = lax.broadcasted_iota(jnp.int32, (16, 64), 0)
    c = lax.broadcasted_iota(jnp.int32, (16, 64), 1)
    h, l0, l1 = (0, 1, 2), (8, 9, 10), (11, 12, 13)
    n0, n1, one, other, m0, m1, m2 = 3, 4, 5, 6, 7, 14, 15
    entries = []
    for k in range(3):
        entries += [(0, h[k], h[k], -2.0)]
        entries += [(1, h[k], l0[k], -2.0), (1, l0[k], h[k], -2.0), (1, l1[k], h[k], -2.0)]
        entries += [(2, h[k], l1[k], -2.0), (2, l0[k], l0[k], -2.0), (2, l1[k], l0[k], -2.0)]
        entries += [(3, l0[k], l1[k], -2.0), (3, l1[k], l1[k], -2.0)]
    entries += [(0, n0, one, 1.0), (0, n1, one, 1.0), (0, one, n0, 1.0), (0, other, n1, 1.0)]
    entries += [(1, m0, one, 1.0), (1, m1, one, 1.0), (1, m2, one, 1.0)]
    entries += [(1, one, m0, 1.0), (1, other, m1, 1.0), (2, one, m2, 1.0)]
    out = jnp.zeros((16, 64), f32)
    for block, source, target, value in entries:
        out = jnp.where((r == target) & (c == 16 * block + source), value, out)
    return out.astype(bf16)


def targets_of(feature_rows, mix):
    return lax.dot_general(feature_rows, mix, TN, preferred_element_type=f32).astype(bf16)


def covariance(squared):
    y = jnp.maximum(squared, TINY)
    return jnp.exp2(y * lax.rsqrt(y) * RATE)


def up_body(coords, charges, bases, up_transfer, top_transfer, tile, first, last):
    leaves = coords.shape[0]
    edge = first.shape[0]
    for ref, start in ((first, 0), (last, leaves - edge)):
        ref[:, 0:3, :] = coords[start : start + edge]
        ref[:, 3:4, :] = jnp.zeros((edge, 1, coords.shape[2]), f32)
        ref[:, 4:8, :] = charges[start : start + edge]
    mids = []
    lift = None
    for n in range(leaves // 8):
        mid = None
        for leaf in range(8 * n, 8 * n + 8):
            coeffs = fold8(dot2(rows8(charges[leaf]), bases[leaf], NT))
            part = fold8(dot2(rows8(coeffs), up_transfer[leaf], NT))
            mid = part if mid is None else mid + part
        mids.append(mid)
        part = fold8(dot2(rows8(mid), top_transfer[n], NT))
        lift = part if lift is None else lift + part
    tile[0:4, :] = jnp.concatenate(mids, axis=1)
    tile[4:8, :] = jnp.concatenate([lift, jnp.zeros_like(lift)], axis=1)


def up_call(coords, charges, bases, up_transfer, top_transfer):
    points = coords.shape[2]
    halo = jax.ShapeDtypeStruct((EDGE, 8, points), f32)
    return pl.pallas_call(
        up_body,
        out_shape=(jax.ShapeDtypeStruct((8, 128), f32), halo, halo),
        in_specs=[VM] * 5,
        out_specs=(VM, VM, VM),
        compiler_params=pltpu.CompilerParams(vmem_limit_bytes=VMEM_LIMIT),
        name="upward",
    )(coords, charges, bases, up_transfer, top_transfer)


def near_body(
    near_list,
    near_count,
    coords,
    charges,
    before,
    after,
    out,
    target_rows,
    source_rows,
    source_vals,
    square_a,
    square_b,
    kern_a,
    kern_b,
    total_rows,
    pair_t,
    pair_s,
    *,
    chunk,
    unroll,
):
    leaves, _, points = coords.shape
    edge = before.shape[0]
    slots = near_list.shape[1]
    window_start = lax.axis_index("leaf") * leaves - edge
    total = 0
    for t in range(leaves):
        for j in range(slots):
            pair_t[total + j] = t
            pair_s[total + j] = near_list[t, j] - window_start
        total = total + near_count[t]
    for j in range(unroll + 1):
        pair_t[total + j] = leaves
        pair_s[total + j] = 0
    mix = mixing()

    def put(slot, pts, vals):
        rows = features(pts)
        for b in range(4):
            source_rows[slot, 16 * b : 16 * b + 16, :] = rows
        source_vals[slot] = rows8(vals)
        return rows

    def own(i, _):
        target_rows[i] = targets_of(put(edge + i, coords[i], charges[i]), mix)
        return 0

    lax.fori_loop(0, leaves, own, 0, unroll=2)

    def halo(i, _):
        put(i, before[i, 0:3, :], before[i, 4:8, :])
        put(edge + leaves + i, after[i, 0:3, :], after[i, 4:8, :])
        return 0

    lax.fori_loop(0, edge, halo, 0)
    target_rows[leaves] = jnp.zeros((points, 64), bf16)
    total_rows[...] = jnp.zeros_like(total_rows)
    kern_b[...] = jnp.zeros_like(kern_b)

    def distances(i, dst, c):
        dst[c : c + chunk, :] = jnp.dot(
            target_rows[pair_t[i], c : c + chunk, :], source_rows[pair_s[i]], preferred_element_type=f32
        )

    def kernels(src, dst, c):
        high, low = split2(covariance(src[c : c + chunk, :]))
        dst[0, c : c + chunk, :] = high
        dst[1, c : c + chunk, :] = low

    def apply(i, src, c):
        vals = source_vals[pair_s[i]]
        total_rows[pair_t[i], :, c : c + chunk] += lax.dot_general(
            vals, src[0, c : c + chunk, :], NT, preferred_element_type=f32
        ) + lax.dot_general(vals, src[1, c : c + chunk, :], NT, preferred_element_type=f32)

    chunks = range(0, points, chunk)
    for c in chunks:
        distances(0, square_a, c)

    def step(k, _):
        i = unroll * k
        previous = jnp.where(k == 0, total, i - 1)
        for u in range(0, unroll, 2):
            for c in chunks:
                kernels(square_a, kern_a, c)
                distances(i + u + 1, square_b, c)
                apply(previous if u == 0 else i + u - 1, kern_b, c)
            for c in chunks:
                kernels(square_b, kern_b, c)
                distances(i + u + 2, square_a, c)
                apply(i + u, kern_a, c)
        return 0

    trips = (total + unroll - 1) // unroll
    lax.fori_loop(0, trips, step, 0)
    for c in chunks:
        apply(unroll * trips - 1, kern_b, c)

    def finish(i, _):
        out[i] = fold8(total_rows[i])
        return 0

    lax.fori_loop(0, leaves, finish, 0, unroll=4)


def near_call(near_list, near_count, coords, charges, before, after, chunk=128, unroll=4):
    leaves, _, points = coords.shape
    window = leaves + 2 * EDGE
    pairs = near_list.shape[1] * leaves + unroll + 4
    return pl.pallas_call(
        functools.partial(near_body, chunk=chunk, unroll=unroll),
        out_shape=jax.ShapeDtypeStruct((leaves, NRHS, points), f32),
        in_specs=[SM, SM, VM, VM, VM, VM],
        out_specs=VM,
        scratch_shapes=[
            pltpu.VMEM((leaves + 1, points, 64), bf16),
            pltpu.VMEM((window, 64, points), bf16),
            pltpu.VMEM((window, 2 * NRHS, points), bf16),
            pltpu.VMEM((points, points), f32),
            pltpu.VMEM((points, points), f32),
            pltpu.VMEM((2, points, points), bf16),
            pltpu.VMEM((2, points, points), bf16),
            pltpu.VMEM((leaves + 1, 2 * NRHS, points), f32),
            pltpu.SMEM((pairs,), jnp.int32),
            pltpu.SMEM((pairs,), jnp.int32),
        ],
        compiler_params=pltpu.CompilerParams(vmem_limit_bytes=VMEM_LIMIT),
        name="near",
    )(near_list, near_count, coords, charges, before, after)


def far_body(
    far_mid,
    mid_count,
    far_top,
    top_count,
    gathered,
    near,
    bases,
    up_transfer,
    top_transfer,
    proxy_mid,
    proxy_top,
    out,
    mid_ids,
    top_ids,
    pts,
    coef,
    sems,
):
    leaves = near.shape[0]
    nodes = leaves // 8
    rank = bases.shape[1]
    device = lax.axis_index("leaf")
    own = device * nodes
    parent = own // 8
    mid_row = (own // 8) * 8
    top_row = (parent // 8) * 8
    copies = (
        pltpu.make_async_copy(far_mid.at[pl.ds(pl.multiple_of(mid_row, 8), 8), :], mid_ids, sems.at[0]),
        pltpu.make_async_copy(far_top.at[pl.ds(pl.multiple_of(top_row, 8), 8), :], top_ids, sems.at[1]),
    )
    for copy in copies:
        copy.start()
    for copy in copies:
        copy.wait()
    mix = mixing()
    lane = lax.broadcasted_iota(jnp.int32, (NRHS, 2 * rank), 1)

    def field(target, ids, row, count, proxy, coeffs_of):
        slots = ids.shape[1]
        for j in range(0, slots, 2):
            a, b = ids[row, j], ids[row, j + 1]
            at = slice(rank * j, rank * j + 2 * rank)
            pts[0:3, at] = jnp.concatenate([proxy[a], proxy[b]], axis=1)
            left = jnp.where(j < count, coeffs_of(a, 0), 0.0)
            right = jnp.where(j + 1 < count, coeffs_of(b, 1), 0.0)
            coef[:, at] = jnp.where(lane < rank, left, right)
        width = rank * slots
        rows = features(pts[0:3, 0:width])
        squared = jnp.dot(
            targets_of(features(target), mix), jnp.concatenate([rows] * 4, axis=0), preferred_element_type=f32
        )
        return fold8(dot2(rows8(coef[:, 0:width]), covariance(squared), NT))

    def mid_coeffs(s, half):
        node = gathered[s // 2, 0:NRHS, :]
        return jnp.where(s % 2 == half, node, pltpu.roll(node, rank, 1))

    def top_coeffs(s, half):
        node = gathered[4 * s, NRHS : 2 * NRHS, :]
        for k in range(1, 4):
            node = node + gathered[4 * s + k, NRHS : 2 * NRHS, :]
        return node if half == 0 else pltpu.roll(node, rank, 1)

    top_field = field(proxy_top[parent], top_ids, parent - top_row, top_count[parent], proxy_top, top_coeffs)
    top8 = rows8(top_field)
    for n in range(nodes):
        mid_field = field(
            proxy_mid[own + n], mid_ids, own - mid_row + n, mid_count[own + n], proxy_mid, mid_coeffs
        )
        mid_field = mid_field + fold8(dot2(top8, top_transfer[n], (((1,), (0,)), ((), ()))))
        mid8 = rows8(mid_field)
        for leaf in range(8 * n, 8 * n + 8):
            leaf_field = fold8(dot2(mid8, up_transfer[leaf], (((1,), (0,)), ((), ()))))
            far = fold8(dot2(rows8(leaf_field), bases[leaf], (((1,), (0,)), ((), ()))))
            out[leaf] = (near[leaf] + far) * out_scale


def far_call(
    far_mid, mid_count, far_top, top_count, gathered, near, bases, up_transfer, top_transfer, proxy_mid, proxy_top
):
    width = bases.shape[1] * max(far_mid.shape[1], far_top.shape[1])
    return pl.pallas_call(
        far_body,
        out_shape=jax.ShapeDtypeStruct(near.shape, f32),
        in_specs=[ANY, SM, ANY, SM] + [VM] * 7,
        out_specs=VM,
        scratch_shapes=[
            pltpu.SMEM((8, far_mid.shape[1]), jnp.int32),
            pltpu.SMEM((8, far_top.shape[1]), jnp.int32),
            pltpu.VMEM((8, width), f32),
            pltpu.VMEM((NRHS, width), f32),
            pltpu.SemaphoreType.DMA((2,)),
        ],
        compiler_params=pltpu.CompilerParams(vmem_limit_bytes=VMEM_LIMIT),
        name="far",
    )(far_mid, mid_count, far_top, top_count, gathered, near, bases, up_transfer, top_transfer, proxy_mid, proxy_top)


def shards(
    coords,
    charges,
    bases,
    up_transfer,
    top_transfer,
    proxy_mid,
    proxy_top,
    near_list,
    near_count,
    far_mid,
    far_mid_count,
    far_top,
    far_top_count,
):
    peers = lax.axis_size("leaf")
    up = [(i, i + 1) for i in range(peers - 1)]
    down = [(j, i) for i, j in up]
    tile, first, last = up_call(coords, charges, bases, up_transfer, top_transfer)
    before = lax.ppermute(last, "leaf", up)
    after = lax.ppermute(first, "leaf", down)
    copies = jnp.broadcast_to(tile, (peers,) + tile.shape)
    gathered = lax.all_to_all(copies, "leaf", 0, 0, tiled=True)
    near = near_call(near_list, near_count, coords, charges, before, after)
    return far_call(
        far_mid,
        far_mid_count,
        far_top,
        far_top_count,
        gathered,
        near,
        bases,
        up_transfer,
        top_transfer,
        proxy_mid,
        proxy_top,
    )


def solution(mesh):
    placed = (
        P("leaf", None, None),
        P("leaf", None, None),
        P("leaf", None, None),
        P("leaf", None, None),
        P("leaf", None, None),
        P(),
        P(),
        P("leaf", None),
        P("leaf"),
        P(),
        P(),
        P(),
        P(),
    )
    return jax.shard_map(
        shards, mesh=mesh, in_specs=placed, out_specs=P("leaf", None, None), check_vma=False
    )
```

time: 211 us -> 71.1 us (0.34)
  the two profiles are of different devices: /device:TPU:1 before, /device:TPU:29 now
where the time goes in v1:
time: 71.1 us; the launch traced here: 70.2 us
  Pallas kernels  43 us (60%)
  starting transfers between devices  15.9 us (22%)
  local copies, waits for them, and re-layouts  8.38 us (12%)
  waiting for transfers between devices  2.89 us (4%)
    pallas_call x1, Pallas kernels, near_call(): pl.pallas_call(functools.partial(near_body, chunk=chunk, unroll=unroll),...  29.7 us
    all_to_all x1, starting transfers between devices, shards(): gathered = lax.all_to_all(copies, 'leaf', 0, 0, tiled=True)  10.5 us
    pallas_call x1, Pallas kernels, far_call(): pl.pallas_call(far_body, out_shape=jax.ShapeDtypeStruct(near.shape, f32),...  7.18 us
    unnamed x22, local copies, waits for them, and re-layouts  6.86 us
    pallas_call x1, Pallas kernels, up_call(): pl.pallas_call(up_body, out_shape=(jax.ShapeDtypeStruct((8, 128), f32), h...  6.1 us
    ppermute x1, starting transfers between devices, shards(): before = lax.ppermute(last, 'leaf', up)  3.43 us
    ppermute x1, waiting for transfers between devices, shards(): after = lax.ppermute(first, 'leaf', down)  2.89 us
    ppermute x1, starting transfers between devices, shards(): after = lax.ppermute(first, 'leaf', down)  1.92 us
  transfers between devices with their start and end apart: 3, of which 1 were waited for; matrix products, arithmetic and copies ran while one was open for 5% of the time, Pallas kernels for 42%

profile of v1, /device:TPU:29, one launch (start us, length us, event | category | flops | bytes accessed | tf_op | source)
XLA Modules:
  0.0 70.2 jit_solution(3348505052869112264)
XLA Ops:
  0.0 1.6 %copy.14.coords = f32[16,3,512]{2,1,0:T(4,128)} copy(f32[16,3,512]{2,0,1:T(8,128)} %param.13) | data formatting | bytes 196608 | tf_op args[0]
  1.6 0.0 copy-start.7
  1.6 0.0 copy-start.6
  1.6 0.0 copy-start.4
  1.6 0.0 copy-start.5
  1.6 0.0 copy-start.1
  1.6 6.1 %upward.1 = (f32[8,128]{1,0:T(8,128)}, f32[8,8,512]{2,1,0:T(8,128)}, f32[8,8,512]{2,1,0:T(8,128)}) custom-call(f32[16,3,512]{2,1,0:T(4,128)} %copy.14.coords, f32[16,4,512]{2,1,0:T(4,128)} %charges.3, f32[16,64,512]{2,1,0:T(8,128)} %bases.3, f32[16,64,64]{2,1,0:T(8,128)} %up_transfer.3, f32[2,64,64]{2,1,0:T(8,128)} %top_transfer.3), custom_call_target="tpu_custom_call" | custom-call | tf_op jit(solution)/shard_map/upward/pallas_call | solution.py:123
  7.7 1.5 %broadcast_in_dim.3 = f32[128,8,128]{2,1,0:T(8,128)} broadcast(f32[8,128]{1,0:T(8,128)} %get-tuple-element.8), dimensions={1,2} | broadcast | bytes 528384 | tf_op jit(solution)/shard_map/broadcast_in_dim | solution.py:385
  9.3 10.5 %all-to-all-start = ((f32[128,8,128]{2,1,0:T(8,128)}), f32[128,8,128]{2,1,0:T(8,128)S(1)}, u32[]{:S(2)}, u32[]{:S(2)}) async-start(f32[128,8,128]{2,1,0:T(8,128)} %broadcast_in_dim.3), calls=%async_computation | async-start | bytes 1048576 | tf_op jit(solution)/shard_map/all_to_all | solution.py:386
  19.8 3.4 %collective-permute-start = (f32[8,8,512]{2,1,0:T(8,128)}, f32[8,8,512]{2,1,0:T(8,128)S(1)}, u32[]{:S(2)}, u32[]{:S(2)}) collective-permute-start(f32[8,8,512]{2,1,0:T(8,128)} %get-tuple-element.9), channel_id=1, source_target_pairs={{0,1},{1,2},{2,3},{3,4},{4,5},{5,6},{6,7},{7,8},{8,9},{9,10},{10,1... | collective-permute-start | bytes 393224 | tf_op jit(solution)/shard_map/ppermute | solution.py:383
  23.2 1.9 %collective-permute-start.1 = (f32[8,8,512]{2,1,0:T(8,128)}, f32[8,8,512]{2,1,0:T(8,128)S(1)}, u32[]{:S(2)}, u32[]{:S(2)}) collective-permute-start(f32[8,8,512]{2,1,0:T(8,128)} %get-tuple-element.10), channel_id=1, source_target_pairs={{1,0},{2,1},{3,2},{4,3},{5,4},{6,5},{7,6},{8,7},{9,8},{10,9},{11,1... | collective-permute-start | bytes 393224 | tf_op jit(solution)/shard_map/ppermute | solution.py:384
  25.2 0.0 copy-done.7
  25.2 0.7 copy.15.near_list
  25.9 0.0 copy-done.6
  25.9 0.7 copy.18.far_top
  26.5 0.0 copy-done.4
  26.5 0.7 copy.20.proxy_top
  27.2 0.0 copy-done.5
  27.2 0.7 %copy.17.far_mid = s32[256,32]{1,0:T(8,128)} copy(s32[256,32]{0,1:T(8,128)S(1)} %copy-done.5) | data formatting | bytes 65536 | tf_op args[9]
  27.9 0.0 copy-done.1
  28.0 1.0 %copy.19.proxy_mid = f32[256,3,64]{2,1,0:T(4,128)} copy(f32[256,3,64]{0,2,1:T(8,128)S(1)} %copy-done.1) | data formatting | bytes 393216 | tf_op args[5]
  29.0 0.0 collective-permute-done.before
  29.0 0.0 copy-start.2
  29.0 2.9 %collective-permute-done.1.after = f32[8,8,512]{2,1,0:T(8,128)S(1)} collective-permute-done((f32[8,8,512]{2,1,0:T(8,128)}, f32[8,8,512]{2,1,0:T(8,128)S(1)}, u32[]{:S(2)}, u32[]{:S(2)}) %collective-permute-start.1) | collective-permute-done | bytes 131104 | tf_op jit(solution)/shard_map/ppermute | solution.py:384
  31.8 0.0 copy-done.2
  31.9 0.0 copy-start.3
  31.9 0.7 copy-done.3
  32.5 29.7 %near.1 = f32[16,4,512]{2,1,0:T(4,128)} custom-call(s32[16,4]{1,0:T(8,128)} %copy.15.near_list, s32[16]{0:T(128)} %near_count.1, f32[16,3,512]{2,1,0:T(4,128)} %copy.14.coords, f32[16,4,512]{2,1,0:T(4,128)} %charges.3, f32[8,8,512]{2,1,0:T(8,128)} %copy-done.2, f32[8,8,512]{2,1,0:T(8,128)} %copy-done.3), custom_call_target="tpu_custom_call" | custom-call | tf_op jit(solution)/shard_map/near/pallas_call | solution.py:243
  62.2 0.0 all-to-all-done.gathered
  62.3 0.0 copy-start
  62.3 0.8 %copy-done = f32[128,8,128]{2,1,0:T(8,128)} copy-done((f32[128,8,128]{2,1,0:T(8,128)}, f32[128,8,128]{2,1,0:T(8,128)S(1)}, u32[]{:S(2)}) %copy-start) | copy-done | bytes 524312
  63.1 7.2 %far.1 = f32[16,4,512]{2,1,0:T(4,128)} custom-call(s32[256,32]{1,0:T(8,128)} %copy.17.far_mid, s32[256]{0:T(256)} %mid_count.1, s32[32,6]{1,0:T(8,128)} %copy.18.far_top, s32[32]{0:T(128)} %top_count.1, f32[128,8,128]{2,1,0:T(8,128)} %copy-done, f32[16,4,512]{2,1,0:T(4,128)} %near.1, f32[16,64,512]{2,1,0:T(8,128)} %bases.3, f32[16,64,64]{2,1,0:T(8,128)} %up_transfer.3, ...), custom_call_target="tpu_custom_call" | custom-call | tf_op jit(solution)/shard_map/far/pallas_call | solution.py:347
Async XLA Ops:
  1.6 23.6 %copy-start.7 = (s32[16,4]{0,1:T(4,128)S(1)}, s32[16,4]{0,1:T(4,128)}, u32[]{:S(2)}) copy-start(s32[16,4]{0,1:T(4,128)} %param.20) | copy-start | bytes 772
  1.6 24.2 %copy-start.6 = (s32[32,6]{0,1:T(8,128)S(1)}, s32[32,6]{0,1:T(8,128)}, u32[]{:S(2)}) copy-start(s32[32,6]{0,1:T(8,128)} %param.24) | copy-start | bytes 2308
  1.6 24.9 %copy-start.4 = (f32[32,3,64]{2,0,1:T(8,128)S(1)}, f32[32,3,64]{2,0,1:T(8,128)}, u32[]{:S(2)}) copy-start(f32[32,3,64]{2,0,1:T(8,128)} %param.19) | copy-start | bytes 73732
  1.6 25.6 %copy-start.5 = (s32[256,32]{0,1:T(8,128)S(1)}, s32[256,32]{0,1:T(8,128)}, u32[]{:S(2)}) copy-start(s32[256,32]{0,1:T(8,128)} %param.22) | copy-start | bytes 98308
  1.6 26.3 %copy-start.1 = (f32[256,3,64]{0,2,1:T(8,128)S(1)}, f32[256,3,64]{0,2,1:T(8,128)}, u32[]{:S(2)}) copy-start(f32[256,3,64]{0,2,1:T(8,128)} %param.18) | copy-start | bytes 589828
  9.3 53.0 %all-to-all-start = ((f32[128,8,128]{2,1,0:T(8,128)}), f32[128,8,128]{2,1,0:T(8,128)S(1)}, u32[]{:S(2)}, u32[]{:S(2)}) async-start(f32[128,8,128]{2,1,0:T(8,128)} %broadcast_in_dim.3), calls=%async_computation | async-start | bytes 1048576 | tf_op jit(solution)/shard_map/all_to_all | solution.py:386
  19.8 9.2 %collective-permute-start = (f32[8,8,512]{2,1,0:T(8,128)}, f32[8,8,512]{2,1,0:T(8,128)S(1)}, u32[]{:S(2)}, u32[]{:S(2)}) collective-permute-start(f32[8,8,512]{2,1,0:T(8,128)} %get-tuple-element.9), channel_id=1, source_target_pairs={{0,1},{1,2},{2,3},{3,4},{4,5},{5,6},{6,7},{7,8},{8,9},{9,10},{10,1... | collective-permute-start | bytes 393224 | tf_op jit(solution)/shard_map/ppermute | solution.py:383
  23.2 8.6 %collective-permute-start.1 = (f32[8,8,512]{2,1,0:T(8,128)}, f32[8,8,512]{2,1,0:T(8,128)S(1)}, u32[]{:S(2)}, u32[]{:S(2)}) collective-permute-start(f32[8,8,512]{2,1,0:T(8,128)} %get-tuple-element.10), channel_id=1, source_target_pairs={{1,0},{2,1},{3,2},{4,3},{5,4},{6,5},{7,6},{8,7},{9,8},{10,9},{11,1... | collective-permute-start | bytes 393224 | tf_op jit(solution)/shard_map/ppermute | solution.py:384
  29.0 2.9 %copy-start.2 = (f32[8,8,512]{2,1,0:T(8,128)}, f32[8,8,512]{2,1,0:T(8,128)S(1)}, u32[]{:S(2)}) copy-start(f32[8,8,512]{2,1,0:T(8,128)S(1)} %collective-permute-done.before) | copy-start | bytes 393220
  31.9 0.7 copy-start.3
  62.3 0.8 %copy-start = (f32[128,8,128]{2,1,0:T(8,128)}, f32[128,8,128]{2,1,0:T(8,128)S(1)}, u32[]{:S(2)}) copy-start(f32[128,8,128]{2,1,0:T(8,128)S(1)} %all-to-all-done.gathered) | copy-start | bytes 1572868

commit v2 on v1

v2 whole, which is shorter than its diff:
```python
import functools

import jax
import jax.numpy as jnp
from jax import lax
from jax.experimental import pallas as pl
from jax.experimental.pallas import tpu as pltpu
from jax.sharding import PartitionSpec as P


EDGE = 8
NRHS = 4
length_scale = 0.4
out_scale = 0.125
TINY = 1e-30
RATE = -1.4426950408889634 / length_scale
NT = (((1,), (1,)), ((), ()))
TN = (((0,), (0,)), ((), ()))
bf16 = jnp.bfloat16
f32 = jnp.float32
VM = pl.BlockSpec(memory_space=pltpu.VMEM)
HBM = pl.BlockSpec(memory_space=pltpu.HBM)
VMEM_LIMIT = 56 * 2**20


def snap(value, magic):
    return (value + magic) - magic


def split2(value):
    high = value.astype(bf16)
    return high, (value - high.astype(f32)).astype(bf16)


def rows8(value):
    high, low = split2(value)
    return jnp.concatenate([high.astype(f32), low.astype(f32)], axis=0).astype(bf16)


def fold8(value):
    return value[0:NRHS] + value[NRHS : 2 * NRHS]


def dot2(rows, value, dims):
    high, low = split2(value)
    return lax.dot_general(rows, high, dims, preferred_element_type=f32) + lax.dot_general(
        rows, low, dims, preferred_element_type=f32
    )


def pieces(x0, x1, x2, put):
    n = m = None
    for k, points in enumerate((x0, x1, x2)):
        x = points - 0.5
        h = snap(x, 49152.0)
        low = x - h
        l0 = snap(low, 96.0)
        put(k, h)
        put(8 + k, l0)
        put(11 + k, low - l0)
        n = h * h if n is None else n + h * h
        part = low * (h + h + low)
        m = part if m is None else m + part
    n0 = snap(n, 49152.0)
    m0 = snap(m, 384.0)
    m1 = snap(m - m0, 1.5)
    for row, value in ((3, n0), (4, n - n0), (7, m0), (14, m1), (15, m - m0 - m1)):
        put(row, value)
    one = jnp.ones_like(n)
    put(5, one)
    put(6, one)


def features(points):
    rows = [None] * 16

    def put(row, value):
        rows[row] = value

    pieces(points[0:1], points[1:2], points[2:3], put)
    return jnp.concatenate(rows, axis=0).astype(bf16)


def mixing():
    r = lax.broadcasted_iota(jnp.int32, (16, 64), 0)
    c = lax.broadcasted_iota(jnp.int32, (16, 64), 1)
    h, l0, l1 = (0, 1, 2), (8, 9, 10), (11, 12, 13)
    n0, n1, one, other, m0, m1, m2 = 3, 4, 5, 6, 7, 14, 15
    entries = []
    for k in range(3):
        entries += [(0, h[k], h[k], -2.0)]
        entries += [(1, h[k], l0[k], -2.0), (1, l0[k], h[k], -2.0), (1, l1[k], h[k], -2.0)]
        entries += [(2, h[k], l1[k], -2.0), (2, l0[k], l0[k], -2.0), (2, l1[k], l0[k], -2.0)]
        entries += [(3, l0[k], l1[k], -2.0), (3, l1[k], l1[k], -2.0)]
    entries += [(0, n0, one, 1.0), (0, n1, one, 1.0), (0, one, n0, 1.0), (0, other, n1, 1.0)]
    entries += [(1, m0, one, 1.0), (1, m1, one, 1.0), (1, m2, one, 1.0)]
    entries += [(1, one, m0, 1.0), (1, other, m1, 1.0), (2, one, m2, 1.0)]
    out = jnp.zeros((16, 64), f32)
    for block, source, target, value in entries:
        out = jnp.where((r == target) & (c == 16 * block + source), value, out)
    return out.astype(bf16)


def targets_of(feature_rows, mix):
    return lax.dot_general(feature_rows, mix, TN, preferred_element_type=f32).astype(bf16)


def covariance(squared):
    y = jnp.maximum(squared, TINY)
    return jnp.exp2(y * lax.rsqrt(y) * RATE)


def up_body(
    coords_hbm,
    charges_hbm,
    bases_hbm,
    up_hbm,
    top_hbm,
    copies_hbm,
    beside_hbm,
    across_hbm,
    coords,
    charges,
    bases,
    up_transfer,
    top_transfer,
    copies,
    beside,
    across,
    sems,
    group_sems,
):
    leaves = charges.shape[0]
    edge = beside.shape[1]
    group = 4
    small = [
        pltpu.make_async_copy(src, dst, sems.at[k])
        for k, (src, dst) in enumerate(((charges_hbm, charges), (coords_hbm, coords), (top_hbm, top_transfer)))
    ]
    moves = []
    for g in range(leaves // group):
        at = pl.ds(group * g, group)
        moves.append(
            (
                pltpu.make_async_copy(bases_hbm.at[at], bases.at[at], group_sems.at[0, g]),
                pltpu.make_async_copy(up_hbm.at[at], up_transfer.at[at], group_sems.at[1, g]),
            )
        )
    for move in small[0:2] + [m for pair in moves for m in pair] + small[2:]:
        move.start()
    small[0].wait()
    small[1].wait()
    odd = lax.axis_index("leaf") % 2
    sends = []
    for k, (ref, start) in enumerate(((beside, (1 - odd) * (leaves - edge)), (across, odd * (leaves - edge)))):
        start = pl.multiple_of(start, edge)
        for c in range(3):
            ref[c] = coords[c, pl.ds(start, edge), :]
        ref[3] = jnp.zeros(ref.shape[1:], f32)
        for g in range(4):
            ref[4 + g, 0:4, :] = charges[start + 2 * g]
            ref[4 + g, 4:8, :] = charges[start + 2 * g + 1]
        sends.append(pltpu.make_async_copy(ref, (beside_hbm, across_hbm)[k], sems.at[3 + k]))
        sends[k].start()
    mids = []
    lift = None
    for n in range(leaves // 8):
        mid = None
        for g in range(2 * n, 2 * n + 2):
            for move in moves[g]:
                move.wait()
            for leaf in range(group * g, group * g + group):
                coeffs = fold8(dot2(rows8(charges[leaf]), bases[leaf], NT))
                part = fold8(dot2(rows8(coeffs), up_transfer[leaf], NT))
                mid = part if mid is None else mid + part
        mids.append(mid)
        if n == 0:
            small[2].wait()
        part = fold8(dot2(rows8(mid), top_transfer[n], NT))
        lift = part if lift is None else lift + part
    tile = jnp.concatenate(
        [jnp.concatenate(mids, axis=1), jnp.concatenate([lift, jnp.zeros_like(lift)], axis=1)], axis=0
    )
    copies[...] = jnp.broadcast_to(tile, copies.shape)
    sends.append(pltpu.make_async_copy(copies, copies_hbm, sems.at[5]))
    sends[2].start()
    for send in sends:
        send.wait()


def up_call(peers, coords, charges, bases, up_transfer, top_transfer):
    halo = (8, EDGE, coords.shape[2])
    copies = (peers, 8, 128)
    args = (coords, charges, bases, up_transfer, top_transfer)
    return pl.pallas_call(
        up_body,
        out_shape=tuple(jax.ShapeDtypeStruct(shape, f32) for shape in (copies, halo, halo)),
        in_specs=[HBM] * 5,
        out_specs=(HBM, HBM, HBM),
        scratch_shapes=[pltpu.VMEM(a.shape, f32) for a in args]
        + [pltpu.VMEM(shape, f32) for shape in (copies, halo, halo)]
        + [pltpu.SemaphoreType.DMA((6,)), pltpu.SemaphoreType.DMA((2, 4))],
        compiler_params=pltpu.CompilerParams(vmem_limit_bytes=VMEM_LIMIT),
        name="upward",
    )(*args)


def near_body(
    list_hbm,
    count_hbm,
    coords_hbm,
    charges_hbm,
    beside,
    across,
    out,
    near_list,
    near_count,
    coords,
    charges,
    target_rows,
    source_rows,
    source_vals,
    feature_rows,
    square_a,
    square_b,
    kern_a,
    kern_b,
    total_rows,
    pair_t,
    pair_s,
    sems,
    *,
    chunk,
    unroll,
):
    leaves, _, points = charges.shape
    edge = beside.shape[1]
    slots = near_list.shape[0]
    pairs_of = ((coords_hbm, coords), (list_hbm, near_list), (count_hbm, near_count), (charges_hbm, charges))
    moves = [pltpu.make_async_copy(src, dst, sems.at[k]) for k, (src, dst) in enumerate(pairs_of)]
    for move in moves:
        move.start()
    window_start = lax.axis_index("leaf") * leaves - edge
    odd = lax.axis_index("leaf") % 2
    beside_at = (1 - odd) * (edge + leaves)
    across_at = odd * (edge + leaves)
    mix = mixing()
    target_rows[leaves] = jnp.zeros((points, 64), bf16)
    total_rows[...] = jnp.zeros_like(total_rows)
    kern_b[...] = jnp.zeros_like(kern_b)
    for move in moves:
        move.wait()
    total = 0
    for t in range(leaves):
        for j in range(slots):
            pair_t[total + j] = t
            pair_s[total + j] = near_list[j, t] - window_start
        total = total + near_count[t]
    for j in range(unroll + 1):
        pair_t[total + j] = leaves
        pair_s[total + j] = 0
    for ref, base, count in ((beside, beside_at, edge), (across, across_at, edge), (coords, edge, leaves)):

        def put(row, value):
            for q in range(points // 128):
                feature_rows.at[q][pl.ds(16 * base + row, count, stride=16), :] = value[:, 128 * q : 128 * q + 128]

        pieces(ref[0], ref[1], ref[2], put)

    def rows_of(slot):
        at = pl.ds(pl.multiple_of(16 * slot, 16), 16)
        rows = jnp.concatenate([feature_rows[q, at, :].astype(bf16) for q in range(points // 128)], axis=1)
        for b in range(4):
            source_rows[slot, 16 * b : 16 * b + 16, :] = rows
        return rows

    def own(i, _):
        target_rows[i] = targets_of(rows_of(edge + i), mix)
        source_vals[edge + i] = rows8(charges[i])
        return 0

    lax.fori_loop(0, leaves, own, 0, unroll=4)

    def halo(g, _):
        for ref, base in ((beside, beside_at), (across, across_at)):
            for k in range(2):
                rows_of(base + 2 * g + k)
                source_vals[base + 2 * g + k] = rows8(ref[4 + g, 4 * k : 4 * k + 4, :])
        return 0

    lax.fori_loop(0, edge // 2, halo, 0)

    def distances(i, dst, c):
        dst[c : c + chunk, :] = jnp.dot(
            target_rows[pair_t[i], c : c + chunk, :], source_rows[pair_s[i]], preferred_element_type=f32
        )

    def kernels(src, dst, c):
        high, low = split2(covariance(src[c : c + chunk, :]))
        dst[0, c : c + chunk, :] = high
        dst[1, c : c + chunk, :] = low

    def apply(i, src, c):
        vals = source_vals[pair_s[i]]
        total_rows[pair_t[i], :, c : c + chunk] += lax.dot_general(
            vals, src[0, c : c + chunk, :], NT, preferred_element_type=f32
        ) + lax.dot_general(vals, src[1, c : c + chunk, :], NT, preferred_element_type=f32)

    chunks = range(0, points, chunk)
    for c in chunks:
        distances(0, square_a, c)

    def step(k, _):
        i = unroll * k
        previous = jnp.where(k == 0, total, i - 1)
        for u in range(0, unroll, 2):
            for c in chunks:
                kernels(square_a, kern_a, c)
                distances(i + u + 1, square_b, c)
                apply(previous if u == 0 else i + u - 1, kern_b, c)
            for c in chunks:
                kernels(square_b, kern_b, c)
                distances(i + u + 2, square_a, c)
                apply(i + u, kern_a, c)
        return 0

    trips = (total + unroll - 1) // unroll
    lax.fori_loop(0, trips, step, 0)
    for c in chunks:
        apply(unroll * trips - 1, kern_b, c)

    def finish(i, _):
        out[i] = fold8(total_rows[i])
        return 0

    lax.fori_loop(0, leaves, finish, 0, unroll=4)


def near_call(near_list, near_count, coords, charges, beside, across, chunk=128, unroll=4):
    leaves, _, points = charges.shape
    window = leaves + 2 * EDGE
    pairs = near_list.shape[0] * leaves + unroll + 4
    return pl.pallas_call(
        functools.partial(near_body, chunk=chunk, unroll=unroll),
        out_shape=jax.ShapeDtypeStruct((leaves, NRHS, points), f32),
        in_specs=[HBM] * 4 + [VM] * 2,
        out_specs=VM,
        scratch_shapes=[
            pltpu.SMEM(near_list.shape, jnp.int32),
            pltpu.SMEM(near_count.shape, jnp.int32),
            pltpu.VMEM(coords.shape, f32),
            pltpu.VMEM(charges.shape, f32),
            pltpu.VMEM((leaves + 1, points, 64), bf16),
            pltpu.VMEM((window, 64, points), bf16),
            pltpu.VMEM((window, 2 * NRHS, points), bf16),
            pltpu.VMEM((points // 128, window * 16, 128), f32),
            pltpu.VMEM((points, points), f32),
            pltpu.VMEM((points, points), f32),
            pltpu.VMEM((2, points, points), bf16),
            pltpu.VMEM((2, points, points), bf16),
            pltpu.VMEM((leaves + 1, 2 * NRHS, points), f32),
            pltpu.SMEM((pairs,), jnp.int32),
            pltpu.SMEM((pairs,), jnp.int32),
            pltpu.SemaphoreType.DMA((4,)),
        ],
        compiler_params=pltpu.CompilerParams(vmem_limit_bytes=VMEM_LIMIT),
        name="near",
    )(near_list, near_count, coords, charges, beside, across)


def far_body(
    far_mid_hbm,
    mid_count_hbm,
    far_top_hbm,
    top_count_hbm,
    proxy_mid_hbm,
    proxy_top_hbm,
    top_hbm,
    up_hbm,
    bases_hbm,
    gathered,
    near,
    out,
    far_mid,
    mid_count,
    far_top,
    top_count,
    proxy_mid,
    proxy_top,
    top_transfer,
    up_transfer,
    bases,
    mid_points,
    top_points,
    pts,
    coef,
    sems,
):
    sources = (
        far_mid_hbm,
        mid_count_hbm,
        far_top_hbm,
        top_count_hbm,
        proxy_mid_hbm,
        proxy_top_hbm,
        top_hbm,
        up_hbm,
        bases_hbm,
    )
    places = (far_mid, mid_count, far_top, top_count, proxy_mid, proxy_top, top_transfer, up_transfer, bases)
    moves = [pltpu.make_async_copy(src, dst, sems.at[k]) for k, (src, dst) in enumerate(zip(sources, places))]
    for move in moves:
        move.start()
    leaves = near.shape[0]
    nodes = leaves // 8
    rank = bases.shape[1]
    device = lax.axis_index("leaf")
    own = device * nodes
    parent = own // 8
    for move in moves[0:6]:
        move.wait()
    for k in range(3):
        mids, tops = proxy_mid[k].T, proxy_top[k]
        mid_points[pl.ds(k, mids.shape[0], stride=4), :] = jnp.concatenate([mids, mids], axis=1)
        top_points[pl.ds(k, tops.shape[0], stride=4), :] = jnp.concatenate([tops, tops], axis=1)

    def proxy(ref, node):
        return ref[pl.ds(4 * node, 3), :]

    mix = mixing()
    lane = lax.broadcasted_iota(jnp.int32, (NRHS, 2 * rank), 1)

    def field(node, ids, count, nodes_points, coeffs_of):
        slots = ids.shape[0]
        for j in range(0, slots, 2):
            a, b = ids[j, node], ids[j + 1, node]
            at = slice(rank * j, rank * j + 2 * rank)
            pts[0:3, at] = jnp.where(lane[0:3] < rank, proxy(nodes_points, a), proxy(nodes_points, b))
            left = jnp.where(j < count, coeffs_of(a, 0), 0.0)
            right = jnp.where(j + 1 < count, coeffs_of(b, 1), 0.0)
            coef[:, at] = jnp.where(lane < rank, left, right)
        width = rank * slots
        rows = features(pts[0:3, 0:width])
        squared = jnp.dot(
            targets_of(features(proxy(nodes_points, node)[:, 0:rank]), mix), jnp.concatenate([rows] * 4, axis=0), preferred_element_type=f32
        )
        return fold8(dot2(rows8(coef[:, 0:width]), covariance(squared), NT))

    def mid_coeffs(s, half):
        node = gathered[s // 2, 0:NRHS, :]
        return jnp.where(s % 2 == half, node, pltpu.roll(node, rank, 1))

    def top_coeffs(s, half):
        node = gathered[4 * s, NRHS : 2 * NRHS, :]
        for k in range(1, 4):
            node = node + gathered[4 * s + k, NRHS : 2 * NRHS, :]
        return node if half == 0 else pltpu.roll(node, rank, 1)

    top_field = field(parent, far_top, top_count[parent], top_points, top_coeffs)
    top8 = rows8(top_field)
    for move in moves[6:]:
        move.wait()
    for n in range(nodes):
        mid_field = field(own + n, far_mid, mid_count[own + n], mid_points, mid_coeffs)
        mid_field = mid_field + fold8(dot2(top8, top_transfer[n], (((1,), (0,)), ((), ()))))
        mid8 = rows8(mid_field)
        for leaf in range(8 * n, 8 * n + 8):
            leaf_field = fold8(dot2(mid8, up_transfer[leaf], (((1,), (0,)), ((), ()))))
            far = fold8(dot2(rows8(leaf_field), bases[leaf], (((1,), (0,)), ((), ()))))
            out[leaf] = (near[leaf] + far) * out_scale


def far_call(
    far_mid, mid_count, far_top, top_count, proxy_mid, proxy_top, top_transfer, up_transfer, bases, gathered, near
):
    width = bases.shape[1] * max(far_mid.shape[0], far_top.shape[0])
    integers = (far_mid, mid_count, far_top, top_count)
    floats = (proxy_mid, proxy_top, top_transfer, up_transfer, bases)
    return pl.pallas_call(
        far_body,
        out_shape=jax.ShapeDtypeStruct(near.shape, f32),
        in_specs=[HBM] * 9 + [VM] * 2,
        out_specs=VM,
        scratch_shapes=[pltpu.SMEM(a.shape, jnp.int32) for a in integers]
        + [pltpu.VMEM(a.shape, f32) for a in floats]
        + [
            pltpu.VMEM((4 * proxy_mid.shape[2], 2 * proxy_mid.shape[1]), f32),
            pltpu.VMEM((4 * proxy_top.shape[1], 2 * proxy_top.shape[2]), f32),
            pltpu.VMEM((8, width), f32),
            pltpu.VMEM((NRHS, width), f32),
            pltpu.SemaphoreType.DMA((9,)),
        ],
        compiler_params=pltpu.CompilerParams(vmem_limit_bytes=VMEM_LIMIT),
        name="far",
    )(*integers, *floats, gathered, near)


def shards(
    coords,
    charges,
    bases,
    up_transfer,
    top_transfer,
    proxy_mid,
    proxy_top,
    near_list,
    near_count,
    far_mid,
    far_mid_count,
    far_top,
    far_top_count,
):
    peers = lax.axis_size("leaf")
    chip = [(i, i ^ 1) for i in range(peers)]
    next_chip = [(i, i + 1 if i % 2 else i - 1) for i in range(1, peers - 1)]
    coords = jnp.transpose(coords, (1, 0, 2))
    copies, beside, across = up_call(peers, coords, charges, bases, up_transfer, top_transfer)
    across = lax.ppermute(across, "leaf", next_chip)
    beside = lax.ppermute(beside, "leaf", chip)
    gathered = lax.all_to_all(copies, "leaf", 0, 0, tiled=True)
    near = near_call(near_list.T, near_count, coords, charges, beside, across)
    return far_call(
        far_mid.T,
        far_mid_count,
        far_top.T,
        far_top_count,
        jnp.transpose(proxy_mid, (1, 2, 0)),
        jnp.transpose(proxy_top, (1, 0, 2)),
        top_transfer,
        up_transfer,
        bases,
        gathered,
        near,
    )


def solution(mesh):
    placed = (
        P("leaf", None, None),
        P("leaf", None, None),
        P("leaf", None, None),
        P("leaf", None, None),
        P("leaf", None, None),
        P(),
        P(),
        P("leaf", None),
        P("leaf"),
        P(),
        P(),
        P(),
        P(),
    )
    return jax.shard_map(
        shards, mesh=mesh, in_specs=placed, out_specs=P("leaf", None, None), check_vma=False
    )
```

time: 71.1 us -> 67 us (0.942)
  the two profiles are of different devices: /device:TPU:29 before, /device:TPU:4 now
where the time goes in v2:
time: 67 us; the launch traced here: 66.7 us
  Pallas kernels  41.4 us (62%)
  starting transfers between devices  18.3 us (27%)
  waiting for transfers between devices  5.56 us (8%)
  local copies, waits for them, and re-layouts  1.44 us (2%)
    pallas_call x1, Pallas kernels, near_call(): pl.pallas_call(functools.partial(near_body, chunk=chunk, unroll=unroll),...  27.7 us
    all_to_all x1, starting transfers between devices, shards(): gathered = lax.all_to_all(copies, 'leaf', 0, 0, tiled=True)  10.5 us
    ppermute x1, starting transfers between devices, shards(): across = lax.ppermute(across, 'leaf', next_chip)  7.56 us
    pallas_call x1, Pallas kernels, far_call(): pl.pallas_call(far_body, out_shape=jax.ShapeDtypeStruct(near.shape, f32),...  7.17 us
    pallas_call x1, Pallas kernels, up_call(): pl.pallas_call(up_body, out_shape=tuple((jax.ShapeDtypeStruct(shape, f32)...  6.57 us
    ppermute x1, waiting for transfers between devices, shards(): across = lax.ppermute(across, 'leaf', next_chip)  5.55 us
    unnamed x6, local copies, waits for them, and re-layouts  1.44 us
  transfers between devices with their start and end apart: 3, of which 1 were waited for; matrix products, arithmetic and copies ran while one was open for 0% of the time, Pallas kernels for 42%

profile of v2, /device:TPU:4, one launch (start us, length us, event | category | flops | bytes accessed | tf_op | source)
XLA Modules:
  0.0 66.7 jit_solution(18067342287659939289)
XLA Ops:
  0.0 6.6 %upward.1 = (f32[128,8,128]{2,1,0:T(8,128)}, f32[8,8,512]{2,1,0:T(8,128)}, f32[8,8,512]{2,1,0:T(8,128)}) custom-call(f32[3,16,512]{2,1,0:T(8,128)} %bitcast.6, f32[16,4,512]{2,1,0:T(4,128)} %charges_hbm.3, f32[16,64,512]{2,1,0:T(8,128)} %bases_hbm.3, f32[16,64,64]{2,1,0:T(8,128)} %up_hbm.3, f32[2,64,64]{2,1,0:T(8,128)} %top_hbm.3), custom_call_target="tpu_custom_call" | custom-call | tf_op jit(solution)/shard_map/upward/pallas_call | solution.py:195
  6.6 10.5 %all-to-all-start = ((f32[128,8,128]{2,1,0:T(8,128)}), f32[128,8,128]{2,1,0:T(8,128)S(1)}, u32[]{:S(2)}, u32[]{:S(2)}) async-start(f32[128,8,128]{2,1,0:T(8,128)} %get-tuple-element.8), calls=%async_computation | async-start | bytes 1048576 | tf_op jit(solution)/shard_map/all_to_all | solution.py:520
  17.1 0.2 collective-permute-start
  17.3 7.6 %collective-permute-start.1 = (f32[8,8,512]{2,1,0:T(8,128)}, f32[8,8,512]{2,1,0:T(8,128)S(1)}, u32[]{:S(2)}, u32[]{:S(2)}) collective-permute-start(f32[8,8,512]{2,1,0:T(8,128)} %get-tuple-element.10), channel_id=1, source_target_pairs={{1,2},{2,1},{3,4},{4,3},{5,6},{6,5},{7,8},{8,7},{9,10},{10,9},{11,... | collective-permute-start | bytes 393224 | tf_op jit(solution)/shard_map/ppermute | solution.py:518
  24.8 0.0 collective-permute-done.beside
  24.9 0.0 copy-start.1
  24.9 5.6 %collective-permute-done.1.across = f32[8,8,512]{2,1,0:T(8,128)S(1)} collective-permute-done((f32[8,8,512]{2,1,0:T(8,128)}, f32[8,8,512]{2,1,0:T(8,128)S(1)}, u32[]{:S(2)}, u32[]{:S(2)}) %collective-permute-start.1) | collective-permute-done | bytes 131104 | tf_op jit(solution)/shard_map/ppermute | solution.py:518
  30.4 0.0 copy-start.2
  30.4 0.0 copy-done.1
  30.4 0.6 copy-done.2
  31.1 27.7 %near.1 = f32[16,4,512]{2,1,0:T(4,128)} custom-call(s32[4,16]{1,0:T(4,128)} %bitcast.12, s32[16]{0:T(128)} %count_hbm.1, f32[3,16,512]{2,1,0:T(8,128)} %bitcast.7, f32[16,4,512]{2,1,0:T(4,128)} %charges_hbm.3, f32[8,8,512]{2,1,0:T(8,128)} %copy-done.1, f32[8,8,512]{2,1,0:T(8,128)} %copy-done.2), custom_call_target="tpu_custom_call" | custom-call | tf_op jit(solution)/shard_map/near/pallas_call | solution.py:343
  58.8 0.0 all-to-all-done.gathered
  58.8 0.0 copy-start
  58.8 0.8 %copy-done = f32[128,8,128]{2,1,0:T(8,128)} copy-done((f32[128,8,128]{2,1,0:T(8,128)}, f32[128,8,128]{2,1,0:T(8,128)S(1)}, u32[]{:S(2)}) %copy-start) | copy-done | bytes 524312
  59.6 7.2 %far.1 = f32[16,4,512]{2,1,0:T(4,128)} custom-call(s32[32,256]{1,0:T(8,128)} %bitcast.10, s32[256]{0:T(256)} %mid_count_hbm.1, s32[6,32]{1,0:T(8,128)} %bitcast.11, s32[32]{0:T(128)} %top_count_hbm.1, f32[3,64,256]{2,1,0:T(8,128)} %bitcast.8, f32[3,32,64]{2,1,0:T(8,128)} %bitcast.9, f32[2,64,64]{2,1,0:T(8,128)} %top_hbm.3, f32[16,64,64]{2,1,0:T(8,128)} %up_hbm.3, ...), custom_call_target="tpu_custom_call" | custom-call | tf_op jit(solution)/shard_map/far/pallas_call | solution.py:479
Async XLA Ops:
  6.6 52.2 %all-to-all-start = ((f32[128,8,128]{2,1,0:T(8,128)}), f32[128,8,128]{2,1,0:T(8,128)S(1)}, u32[]{:S(2)}, u32[]{:S(2)}) async-start(f32[128,8,128]{2,1,0:T(8,128)} %get-tuple-element.8), calls=%async_computation | async-start | bytes 1048576 | tf_op jit(solution)/shard_map/all_to_all | solution.py:520
  17.1 7.8 %collective-permute-start = (f32[8,8,512]{2,1,0:T(8,128)}, f32[8,8,512]{2,1,0:T(8,128)S(1)}, u32[]{:S(2)}, u32[]{:S(2)}) collective-permute-start(f32[8,8,512]{2,1,0:T(8,128)} %get-tuple-element.9), channel_id=1, source_target_pairs={{0,1},{1,0},{2,3},{3,2},{4,5},{5,4},{6,7},{7,6},{8,9},{9,8},{10,11... | collective-permute-start | bytes 393224 | tf_op jit(solution)/shard_map/ppermute | solution.py:519
  17.3 13.1 %collective-permute-start.1 = (f32[8,8,512]{2,1,0:T(8,128)}, f32[8,8,512]{2,1,0:T(8,128)S(1)}, u32[]{:S(2)}, u32[]{:S(2)}) collective-permute-start(f32[8,8,512]{2,1,0:T(8,128)} %get-tuple-element.10), channel_id=1, source_target_pairs={{1,2},{2,1},{3,4},{4,3},{5,6},{6,5},{7,8},{8,7},{9,10},{10,9},{11,... | collective-permute-start | bytes 393224 | tf_op jit(solution)/shard_map/ppermute | solution.py:518
  24.9 5.6 %copy-start.1 = (f32[8,8,512]{2,1,0:T(8,128)}, f32[8,8,512]{2,1,0:T(8,128)S(1)}, u32[]{:S(2)}) copy-start(f32[8,8,512]{2,1,0:T(8,128)S(1)} %collective-permute-done.beside) | copy-start | bytes 393220
  30.4 0.6 copy-start.2
  58.8 0.8 %copy-start = (f32[128,8,128]{2,1,0:T(8,128)}, f32[128,8,128]{2,1,0:T(8,128)S(1)}, u32[]{:S(2)}) copy-start(f32[128,8,128]{2,1,0:T(8,128)S(1)} %all-to-all-done.gathered) | copy-start | bytes 1572868

commit v3 on v2

--- a/solution.py
+++ b/solution.py
@@ -20,7 +20,8 @@
 f32 = jnp.float32
 VM = pl.BlockSpec(memory_space=pltpu.VMEM)
 HBM = pl.BlockSpec(memory_space=pltpu.HBM)
-VMEM_LIMIT = 56 * 2**20
+VMEM_LIMIT = 67043328
+BLOCK = 128
 
 
 def snap(value, magic):
@@ -232,6 +233,8 @@
     *,
     chunk,
     unroll,
+    self_unroll,
+    own_unroll,
 ):
     leaves, _, points = charges.shape
     edge = beside.shape[1]
@@ -245,17 +248,14 @@
     beside_at = (1 - odd) * (edge + leaves)
     across_at = odd * (edge + leaves)
     mix = mixing()
-    target_rows[leaves] = jnp.zeros((points, 64), bf16)
-    total_rows[...] = jnp.zeros_like(total_rows)
-    kern_b[...] = jnp.zeros_like(kern_b)
     for move in moves:
         move.wait()
     total = 0
     for t in range(leaves):
-        for j in range(slots):
-            pair_t[total + j] = t
-            pair_s[total + j] = near_list[j, t] - window_start
-        total = total + near_count[t]
+        for j in range(1, slots):
+            pair_t[total + j - 1] = t
+            pair_s[total + j - 1] = near_list[j, t] - window_start
+        total = total + near_count[t] - 1
     for j in range(unroll + 1):
         pair_t[total + j] = leaves
         pair_s[total + j] = 0
@@ -279,7 +279,7 @@
         source_vals[edge + i] = rows8(charges[i])
         return 0
 
-    lax.fori_loop(0, leaves, own, 0, unroll=4)
+    lax.fori_loop(0, leaves, own, 0, unroll=own_unroll)
 
     def halo(g, _):
         for ref, base in ((beside, beside_at), (across, across_at)):
@@ -306,9 +306,50 @@
             vals, src[0, c : c + chunk, :], NT, preferred_element_type=f32
         ) + lax.dot_general(vals, src[1, c : c + chunk, :], NT, preferred_element_type=f32)
 
+    def self_distances(t, dst, c):
+        rows = slice(c, c + BLOCK)
+        dst[rows, c:] = jnp.dot(target_rows[t, rows, :], source_rows[edge + t, :, c:], preferred_element_type=f32)
+
+    def self_kernels(src, dst, c):
+        high, low = split2(covariance(src[c : c + BLOCK, c:]))
+        dst[0, c : c + BLOCK, c:] = high
+        dst[1, c : c + BLOCK, c:] = low
+
+    def self_apply(t, src):
+        vals = source_vals[edge + t]
+        sums = []
+        for c in blocks:
+            part = None
+            for p in range(2):
+                term = lax.dot_general(vals[:, c:], src[p, c : c + BLOCK, c:], NT, preferred_element_type=f32)
+                part = term if part is None else part + term
+                if c:
+                    part += jnp.dot(vals[:, :c], src[p, :c, c : c + BLOCK], preferred_element_type=f32)
+            sums.append(part)
+        total_rows[t] = jnp.concatenate(sums, axis=1)
+
+    blocks = range(0, points, BLOCK)
+    for c in blocks:
+        self_distances(0, square_a, c)
+
+    def self_step(k, _):
+        i = self_unroll * k
+        for u in range(0, self_unroll, 2):
+            for c in blocks:
+                self_kernels(square_a, kern_a, c)
+                self_distances(i + u + 1, square_b, c)
+            self_apply(jnp.where(k == 0, leaves, i - 1) if u == 0 else i + u - 1, kern_b)
+            for c in blocks:
+                self_kernels(square_b, kern_b, c)
+                self_distances(i + u + 2, square_a, c)
+            self_apply(i + u, kern_a)
+        return 0
+
+    lax.fori_loop(0, leaves // self_unroll, self_step, 0)
     chunks = range(0, points, chunk)
     for c in chunks:
         distances(0, square_a, c)
+    self_apply(leaves - 1, kern_b)
 
     def step(k, _):
         i = unroll * k
@@ -327,7 +368,7 @@
     trips = (total + unroll - 1) // unroll
     lax.fori_loop(0, trips, step, 0)
     for c in chunks:
-        apply(unroll * trips - 1, kern_b, c)
+        apply(jnp.maximum(unroll * trips - 1, 0), kern_b, c)
 
     def finish(i, _):
         out[i] = fold8(total_rows[i])
@@ -336,12 +377,12 @@
     lax.fori_loop(0, leaves, finish, 0, unroll=4)
 
 
-def near_call(near_list, near_count, coords, charges, beside, across, chunk=128, unroll=4):
+def near_call(near_list, near_count, coords, charges, beside, across, chunk=128, unroll=2, self_unroll=2, own_unroll=4):
     leaves, _, points = charges.shape
     window = leaves + 2 * EDGE
     pairs = near_list.shape[0] * leaves + unroll + 4
     return pl.pallas_call(
-        functools.partial(near_body, chunk=chunk, unroll=unroll),
+        functools.partial(near_body, chunk=chunk, unroll=unroll, self_unroll=self_unroll, own_unroll=own_unroll),
         out_shape=jax.ShapeDtypeStruct((leaves, NRHS, points), f32),
         in_specs=[HBM] * 4 + [VM] * 2,
         out_specs=VM,
@@ -378,8 +419,8 @@
     top_hbm,
     up_hbm,
     bases_hbm,
-    gathered,
-    near,
+    gathered_hbm,
+    near_hbm,
     out,
     far_mid,
     mid_count,
@@ -390,10 +431,13 @@
     top_transfer,
     up_transfer,
     bases,
+    gathered,
+    near,
     mid_points,
     top_points,
     pts,
     coef,
+    kern,
     sems,
 ):
     sources = (
@@ -403,11 +447,14 @@
         top_count_hbm,
         proxy_mid_hbm,
         proxy_top_hbm,
+        gathered_hbm,
         top_hbm,
         up_hbm,
         bases_hbm,
+        near_hbm,
     )
-    places = (far_mid, mid_count, far_top, top_count, proxy_mid, proxy_top, top_transfer, up_transfer, bases)
+    inputs = (far_mid, mid_count, far_top, top_count, proxy_mid, proxy_top)
+    places = inputs + (gathered, top_transfer, up_transfer, bases, near)
     moves = [pltpu.make_async_copy(src, dst, sems.at[k]) for k, (src, dst) in enumerate(zip(sources, places))]
     for move in moves:
         move.start()
@@ -417,6 +464,7 @@
     device = lax.axis_index("leaf")
     own = device * nodes
     parent = own // 8
+    mix = mixing()
     for move in moves[0:6]:
         move.wait()
     for k in range(3):
@@ -427,28 +475,42 @@
     def proxy(ref, node):
         return ref[pl.ds(4 * node, 3), :]
 
-    mix = mixing()
     lane = lax.broadcasted_iota(jnp.int32, (NRHS, 2 * rank), 1)
 
-    def field(node, ids, count, nodes_points, coeffs_of):
+    def kernels_of(k, node, ids, nodes_points):
         slots = ids.shape[0]
+        width = rank * slots
         for j in range(0, slots, 2):
             a, b = ids[j, node], ids[j + 1, node]
-            at = slice(rank * j, rank * j + 2 * rank)
-            pts[0:3, at] = jnp.where(lane[0:3] < rank, proxy(nodes_points, a), proxy(nodes_points, b))
-            left = jnp.where(j < count, coeffs_of(a, 0), 0.0)
-            right = jnp.where(j + 1 < count, coeffs_of(b, 1), 0.0)
-            coef[:, at] = jnp.where(lane < rank, left, right)
+            pts[k, 0:3, rank * j : rank * j + 2 * rank] = jnp.where(
+                lane[0:3] < rank, proxy(nodes_points, a), proxy(nodes_points, b)
+            )
+        rows = features(pts[k, 0:3, 0:width])
+        squared = jnp.dot(
+            targets_of(features(proxy(nodes_points, node)[:, 0:rank]), mix),
+            jnp.concatenate([rows] * 4, axis=0),
+            preferred_element_type=f32,
+        )
+        high, low = split2(covariance(squared))
+        kern[k, 0, :, 0:width] = high
+        kern[k, 1, :, 0:width] = low
+
+    def field(k, node, ids, count, coeffs_of):
+        slots = ids.shape[0]
         width = rank * slots
-        rows = features(pts[0:3, 0:width])
-        squared = jnp.dot(
-            targets_of(features(proxy(nodes_points, node)[:, 0:rank]), mix), jnp.concatenate([rows] * 4, axis=0), preferred_element_type=f32
+        for j in range(0, slots, 2):
+            left = jnp.where(j < count, coeffs_of(ids[j, node], 0), 0.0)
+            right = jnp.where(j + 1 < count, coeffs_of(ids[j + 1, node], 1), 0.0)
+            coef[k, :, rank * j : rank * j + 2 * rank] = jnp.where(lane < rank, left, right)
+        vals = rows8(coef[k, :, 0:width])
+        return fold8(
+            lax.dot_general(vals, kern[k, 0, :, 0:width], NT, preferred_element_type=f32)
+            + lax.dot_general(vals, kern[k, 1, :, 0:width], NT, preferred_element_type=f32)
         )
-        return fold8(dot2(rows8(coef[:, 0:width]), covariance(squared), NT))
 
     def mid_coeffs(s, half):
-        node = gathered[s // 2, 0:NRHS, :]
-        return jnp.where(s % 2 == half, node, pltpu.roll(node, rank, 1))
+        node = gathered[lax.shift_right_logical(s, 1), 0:NRHS, :]
+        return jnp.where((s & 1) == half, node, pltpu.roll(node, rank, 1))
 
     def top_coeffs(s, half):
         node = gathered[4 * s, NRHS : 2 * NRHS, :]
@@ -456,12 +518,14 @@
             node = node + gathered[4 * s + k, NRHS : 2 * NRHS, :]
         return node if half == 0 else pltpu.roll(node, rank, 1)
 
-    top_field = field(parent, far_top, top_count[parent], top_points, top_coeffs)
-    top8 = rows8(top_field)
+    kernels_of(nodes, parent, far_top, top_points)
+    for n in range(nodes):
+        kernels_of(n, own + n, far_mid, mid_points)
     for move in moves[6:]:
         move.wait()
+    top8 = rows8(field(nodes, parent, far_top, top_count[parent], top_coeffs))
     for n in range(nodes):
-        mid_field = field(own + n, far_mid, mid_count[own + n], mid_points, mid_coeffs)
+        mid_field = field(n, own + n, far_mid, mid_count[own + n], mid_coeffs)
         mid_field = mid_field + fold8(dot2(top8, top_transfer[n], (((1,), (0,)), ((), ()))))
         mid8 = rows8(mid_field)
         for leaf in range(8 * n, 8 * n + 8):
@@ -475,24 +539,26 @@
 ):
     width = bases.shape[1] * max(far_mid.shape[0], far_top.shape[0])
     integers = (far_mid, mid_count, far_top, top_count)
-    floats = (proxy_mid, proxy_top, top_transfer, up_transfer, bases)
+    floats = (proxy_mid, proxy_top, top_transfer, up_transfer, bases, gathered, near)
+    fields = near.shape[0] // 8 + 1
     return pl.pallas_call(
         far_body,
         out_shape=jax.ShapeDtypeStruct(near.shape, f32),
-        in_specs=[HBM] * 9 + [VM] * 2,
+        in_specs=[HBM] * 11,
         out_specs=VM,
         scratch_shapes=[pltpu.SMEM(a.shape, jnp.int32) for a in integers]
         + [pltpu.VMEM(a.shape, f32) for a in floats]
         + [
             pltpu.VMEM((4 * proxy_mid.shape[2], 2 * proxy_mid.shape[1]), f32),
             pltpu.VMEM((4 * proxy_top.shape[1], 2 * proxy_top.shape[2]), f32),
-            pltpu.VMEM((8, width), f32),
-            pltpu.VMEM((NRHS, width), f32),
-            pltpu.SemaphoreType.DMA((9,)),
+            pltpu.VMEM((fields, 8, width), f32),
+            pltpu.VMEM((fields, NRHS, width), f32),
+            pltpu.VMEM((fields, 2, bases.shape[1], width), bf16),
+            pltpu.SemaphoreType.DMA((11,)),
         ],
         compiler_params=pltpu.CompilerParams(vmem_limit_bytes=VMEM_LIMIT),
         name="far",
-    )(*integers, *floats, gathered, near)
+    )(*integers, *floats)
 
 
 def shards(

time: 67 us -> 65.5 us (0.978)
  local copies, waits for them, and re-layouts: 1.44 us -> 0 us
    unnamed x6 -> x0, local copies, waits for them, and re-layouts: 1.44 us -> none
    pallas_call x1, Pallas kernels: 7.17 us -> 5.92 us  [far_call(): pl.pallas_call(far_body, out_shape=jax.ShapeDtypeStruct(near.shape, f32),...]
    pallas_call x1, Pallas kernels: 27.7 us -> 28.9 us  [near_call(): pl.pallas_call(functools.partial(near_body, chunk=chunk, unroll=unroll, s...]
  transfers between devices with their start and end apart: 3 -> 3, of which waited for: 1 -> 1; matrix products, arithmetic and copies ran while one was open for 0% -> 0% of each run, Pallas kernels for 42% -> 44%
where the time goes in v3:
time: 65.5 us; the launch traced here: 65.3 us
  Pallas kernels  41.3 us (63%)
  starting transfers between devices  18.7 us (29%)
  waiting for transfers between devices  5.17 us (8%)
    pallas_call x1, Pallas kernels, near_call(): pl.pallas_call(functools.partial(near_body, chunk=chunk, unroll=unroll, s...  28.9 us
    all_to_all x1, starting transfers between devices, shards(): gathered = lax.all_to_all(copies, 'leaf', 0, 0, tiled=True)  11 us
    ppermute x1, starting transfers between devices, shards(): across = lax.ppermute(across, 'leaf', next_chip)  7.56 us
    pallas_call x1, Pallas kernels, up_call(): pl.pallas_call(up_body, out_shape=tuple((jax.ShapeDtypeStruct(shape, f32)...  6.57 us
    pallas_call x1, Pallas kernels, far_call(): pl.pallas_call(far_body, out_shape=jax.ShapeDtypeStruct(near.shape, f32),...  5.92 us
    ppermute x1, waiting for transfers between devices, shards(): across = lax.ppermute(across, 'leaf', next_chip)  5.17 us
  transfers between devices with their start and end apart: 3, of which 1 were waited for; matrix products, arithmetic and copies ran while one was open for 0% of the time, Pallas kernels for 44%

profile of v3, /device:TPU:4, one launch (start us, length us, event | category | flops | bytes accessed | tf_op | source)
XLA Modules:
  0.0 65.3 jit_solution(6148892198572314781)
XLA Ops:
  0.0 6.6 %upward.1 = (f32[128,8,128]{2,1,0:T(8,128)}, f32[8,8,512]{2,1,0:T(8,128)}, f32[8,8,512]{2,1,0:T(8,128)}) custom-call(f32[3,16,512]{2,1,0:T(8,128)} %bitcast.6, f32[16,4,512]{2,1,0:T(4,128)} %charges_hbm.3, f32[16,64,512]{2,1,0:T(8,128)} %bases_hbm.3, f32[16,64,64]{2,1,0:T(8,128)} %up_hbm.3, f32[2,64,64]{2,1,0:T(8,128)} %top_hbm.3), custom_call_target="tpu_custom_call" | custom-call | tf_op jit(solution)/shard_map/upward/pallas_call | solution.py:196
  6.6 11.0 %all-to-all-start = ((f32[128,8,128]{2,1,0:T(8,128)}), f32[128,8,128]{2,1,0:T(8,128)}, u32[]{:S(2)}, u32[]{:S(2)}) async-start(f32[128,8,128]{2,1,0:T(8,128)} %get-tuple-element.8), calls=%async_computation | async-start | bytes 1048576 | tf_op jit(solution)/shard_map/all_to_all | solution.py:586
  17.6 0.2 collective-permute-start
  17.8 7.6 %collective-permute-start.1 = (f32[8,8,512]{2,1,0:T(8,128)}, f32[8,8,512]{2,1,0:T(8,128)}, u32[]{:S(2)}, u32[]{:S(2)}) collective-permute-start(f32[8,8,512]{2,1,0:T(8,128)} %get-tuple-element.10), channel_id=1, source_target_pairs={{1,2},{2,1},{3,4},{4,3},{5,6},{6,5},{7,8},{8,7},{9,10},{10,9},{11,... | collective-permute-start | bytes 393224 | tf_op jit(solution)/shard_map/ppermute | solution.py:584
  25.3 0.0 collective-permute-done.beside
  25.3 5.2 %collective-permute-done.1.across = f32[8,8,512]{2,1,0:T(8,128)} collective-permute-done((f32[8,8,512]{2,1,0:T(8,128)}, f32[8,8,512]{2,1,0:T(8,128)}, u32[]{:S(2)}, u32[]{:S(2)}) %collective-permute-start.1) | collective-permute-done | bytes 131104 | tf_op jit(solution)/shard_map/ppermute | solution.py:584
  30.5 28.9 %near.1.near_hbm = f32[16,4,512]{2,1,0:T(4,128)} custom-call(s32[4,16]{1,0:T(4,128)} %bitcast.12, s32[16]{0:T(128)} %count_hbm.1, f32[3,16,512]{2,1,0:T(8,128)} %bitcast.7, f32[16,4,512]{2,1,0:T(4,128)} %charges_hbm.3, f32[8,8,512]{2,1,0:T(8,128)} %collective-permute-done.beside, f32[8,8,512]{2,1,0:T(8,128)} %collective-permute-done.1.across), custom_call_target="tpu_custom_call" | custom-call | tf_op jit(solution)/shard_map/near/pallas_call | solution.py:384
  59.4 0.0 all-to-all-done.gathered_hbm
  59.4 5.9 %far.1 = f32[16,4,512]{2,1,0:T(4,128)} custom-call(s32[32,256]{1,0:T(8,128)} %bitcast.10, s32[256]{0:T(256)} %mid_count_hbm.1, s32[6,32]{1,0:T(8,128)} %bitcast.11, s32[32]{0:T(128)} %top_count_hbm.1, f32[3,64,256]{2,1,0:T(8,128)} %bitcast.8, f32[3,32,64]{2,1,0:T(8,128)} %bitcast.9, f32[2,64,64]{2,1,0:T(8,128)} %top_hbm.3, f32[16,64,64]{2,1,0:T(8,128)} %up_hbm.3, ...), custom_call_target="tpu_custom_call" | custom-call | tf_op jit(solution)/shard_map/far/pallas_call | solution.py:544
Async XLA Ops:
  6.6 52.8 %all-to-all-start = ((f32[128,8,128]{2,1,0:T(8,128)}), f32[128,8,128]{2,1,0:T(8,128)}, u32[]{:S(2)}, u32[]{:S(2)}) async-start(f32[128,8,128]{2,1,0:T(8,128)} %get-tuple-element.8), calls=%async_computation | async-start | bytes 1048576 | tf_op jit(solution)/shard_map/all_to_all | solution.py:586
  17.6 7.8 %collective-permute-start = (f32[8,8,512]{2,1,0:T(8,128)}, f32[8,8,512]{2,1,0:T(8,128)}, u32[]{:S(2)}, u32[]{:S(2)}) collective-permute-start(f32[8,8,512]{2,1,0:T(8,128)} %get-tuple-element.9), channel_id=1, source_target_pairs={{0,1},{1,0},{2,3},{3,2},{4,5},{5,4},{6,7},{7,6},{8,9},{9,8},{10,11... | collective-permute-start | bytes 393224 | tf_op jit(solution)/shard_map/ppermute | solution.py:585
  17.8 12.7 %collective-permute-start.1 = (f32[8,8,512]{2,1,0:T(8,128)}, f32[8,8,512]{2,1,0:T(8,128)}, u32[]{:S(2)}, u32[]{:S(2)}) collective-permute-start(f32[8,8,512]{2,1,0:T(8,128)} %get-tuple-element.10), channel_id=1, source_target_pairs={{1,2},{2,1},{3,4},{4,3},{5,6},{6,5},{7,8},{8,7},{9,10},{10,9},{11,... | collective-permute-start | bytes 393224 | tf_op jit(solution)/shard_map/ppermute | solution.py:584

commit v4 on v2

--- a/solution.py
+++ b/solution.py
@@ -20,7 +20,8 @@
 f32 = jnp.float32
 VM = pl.BlockSpec(memory_space=pltpu.VMEM)
 HBM = pl.BlockSpec(memory_space=pltpu.HBM)
-VMEM_LIMIT = 56 * 2**20
+VMEM_LIMIT = 67043328
+BLOCK = 128
 
 
 def snap(value, magic):
@@ -110,6 +111,22 @@
     return jnp.exp2(y * lax.rsqrt(y) * RATE)
 
 
+def spread(ref, base, count, feature_rows):
+    def put(row, value):
+        for q in range(feature_rows.shape[0]):
+            feature_rows.at[q][pl.ds(16 * base + row, count, stride=16), :] = value[:, 128 * q : 128 * q + 128]
+
+    pieces(ref[0], ref[1], ref[2], put)
+
+
+def source_of(slot, feature_rows, source_rows):
+    at = pl.ds(pl.multiple_of(16 * slot, 16), 16)
+    rows = jnp.concatenate([feature_rows[q, at, :].astype(bf16) for q in range(feature_rows.shape[0])], axis=1)
+    for b in range(4):
+        source_rows[slot, 16 * b : 16 * b + 16, :] = rows
+    return rows
+
+
 def up_body(
     coords_hbm,
     charges_hbm,
@@ -119,6 +136,7 @@
     copies_hbm,
     beside_hbm,
     across_hbm,
+    self_hbm,
     coords,
     charges,
     bases,
@@ -127,12 +145,25 @@
     copies,
     beside,
     across,
+    self_part,
+    target_rows,
+    source_rows,
+    source_vals,
+    feature_rows,
+    square_a,
+    square_b,
+    kern_a,
+    kern_b,
+    total_rows,
     sems,
     group_sems,
+    *,
+    self_unroll,
 ):
-    leaves = charges.shape[0]
+    leaves, _, points = charges.shape
     edge = beside.shape[1]
     group = 4
+    mix = mixing()
     small = [
         pltpu.make_async_copy(src, dst, sems.at[k])
         for k, (src, dst) in enumerate(((charges_hbm, charges), (coords_hbm, coords), (top_hbm, top_transfer)))
@@ -162,6 +193,61 @@
             ref[4 + g, 4:8, :] = charges[start + 2 * g + 1]
         sends.append(pltpu.make_async_copy(ref, (beside_hbm, across_hbm)[k], sems.at[3 + k]))
         sends[k].start()
+    spread(coords, 0, leaves, feature_rows)
+
+    def own(i, _):
+        target_rows[i] = targets_of(source_of(i, feature_rows, source_rows), mix)
+        source_vals[i] = rows8(charges[i])
+        return 0
+
+    lax.fori_loop(0, leaves, own, 0, unroll=4)
+
+    def self_distances(t, dst, c):
+        rows = slice(c, c + BLOCK)
+        dst[rows, c:] = jnp.dot(target_rows[t, rows, :], source_rows[t, :, c:], preferred_element_type=f32)
+
+    def self_kernels(src, dst, c):
+        high, low = split2(covariance(src[c : c + BLOCK, c:]))
+        dst[0, c : c + BLOCK, c:] = high
+        dst[1, c : c + BLOCK, c:] = low
+
+    def self_apply(t, src):
+        vals = source_vals[t]
+        sums = []
+        for c in blocks:
+            part = None
+            for p in range(2):
+                term = lax.dot_general(vals[:, c:], src[p, c : c + BLOCK, c:], NT, preferred_element_type=f32)
+                part = term if part is None else part + term
+                if c:
+                    part += jnp.dot(vals[:, :c], src[p, :c, c : c + BLOCK], preferred_element_type=f32)
+            sums.append(part)
+        total_rows[t] = jnp.concatenate(sums, axis=1)
+
+    blocks = range(0, points, BLOCK)
+    for c in blocks:
+        self_distances(0, square_a, c)
+
+    def self_step(k, _):
+        i = self_unroll * k
+        for u in range(0, self_unroll, 2):
+            for c in blocks:
+                self_kernels(square_a, kern_a, c)
+                self_distances(i + u + 1, square_b, c)
+            self_apply(jnp.where(k == 0, leaves, i - 1) if u == 0 else i + u - 1, kern_b)
+            for c in blocks:
+                self_kernels(square_b, kern_b, c)
+                self_distances(i + u + 2, square_a, c)
+            self_apply(i + u, kern_a)
+        return 0
+
+    lax.fori_loop(0, leaves // self_unroll, self_step, 0)
+    self_apply(leaves - 1, kern_b)
+
+    for leaf in range(leaves):
+        self_part[leaf] = fold8(total_rows[leaf])
+    sends.append(pltpu.make_async_copy(self_part, self_hbm, sems.at[6]))
+    sends[2].start()
     mids = []
     lift = None
     for n in range(leaves // 8):
@@ -183,23 +269,35 @@
     )
     copies[...] = jnp.broadcast_to(tile, copies.shape)
     sends.append(pltpu.make_async_copy(copies, copies_hbm, sems.at[5]))
-    sends[2].start()
+    sends[3].start()
     for send in sends:
         send.wait()
 
 
-def up_call(peers, coords, charges, bases, up_transfer, top_transfer):
-    halo = (8, EDGE, coords.shape[2])
+def up_call(peers, coords, charges, bases, up_transfer, top_transfer, self_unroll=2):
+    leaves, _, points = charges.shape
+    halo = (8, EDGE, points)
     copies = (peers, 8, 128)
     args = (coords, charges, bases, up_transfer, top_transfer)
     return pl.pallas_call(
-        up_body,
-        out_shape=tuple(jax.ShapeDtypeStruct(shape, f32) for shape in (copies, halo, halo)),
+        functools.partial(up_body, self_unroll=self_unroll),
+        out_shape=tuple(jax.ShapeDtypeStruct(shape, f32) for shape in (copies, halo, halo, charges.shape)),
         in_specs=[HBM] * 5,
-        out_specs=(HBM, HBM, HBM),
+        out_specs=(HBM,) * 4,
         scratch_shapes=[pltpu.VMEM(a.shape, f32) for a in args]
-        + [pltpu.VMEM(shape, f32) for shape in (copies, halo, halo)]
-        + [pltpu.SemaphoreType.DMA((6,)), pltpu.SemaphoreType.DMA((2, 4))],
+        + [pltpu.VMEM(shape, f32) for shape in (copies, halo, halo, charges.shape)]
+        + [
+            pltpu.VMEM((leaves + 1, points, 64), bf16),
+            pltpu.VMEM((leaves + 1, 64, points), bf16),
+            pltpu.VMEM((leaves + 1, 2 * NRHS, points), bf16),
+            pltpu.VMEM((points // 128, leaves * 16, 128), f32),
+            pltpu.VMEM((points, points), f32),
+            pltpu.VMEM((points, points), f32),
+            pltpu.VMEM((2, points, points), bf16),
+            pltpu.VMEM((2, points, points), bf16),
+            pltpu.VMEM((leaves + 1, 2 * NRHS, points), f32),
+        ]
+        + [pltpu.SemaphoreType.DMA((7,)), pltpu.SemaphoreType.DMA((2, 4))],
         compiler_params=pltpu.CompilerParams(vmem_limit_bytes=VMEM_LIMIT),
         name="upward",
     )(*args)
@@ -210,6 +308,7 @@
     count_hbm,
     coords_hbm,
     charges_hbm,
+    self_hbm,
     beside,
     across,
     out,
@@ -217,6 +316,7 @@
     near_count,
     coords,
     charges,
+    self_part,
     target_rows,
     source_rows,
     source_vals,
@@ -232,11 +332,13 @@
     *,
     chunk,
     unroll,
+    own_unroll,
 ):
     leaves, _, points = charges.shape
     edge = beside.shape[1]
     slots = near_list.shape[0]
     pairs_of = ((coords_hbm, coords), (list_hbm, near_list), (count_hbm, near_count), (charges_hbm, charges))
+    pairs_of += ((self_hbm, self_part),)
     moves = [pltpu.make_async_copy(src, dst, sems.at[k]) for k, (src, dst) in enumerate(pairs_of)]
     for move in moves:
         move.start()
@@ -245,46 +347,33 @@
     beside_at = (1 - odd) * (edge + leaves)
     across_at = odd * (edge + leaves)
     mix = mixing()
-    target_rows[leaves] = jnp.zeros((points, 64), bf16)
     total_rows[...] = jnp.zeros_like(total_rows)
-    kern_b[...] = jnp.zeros_like(kern_b)
     for move in moves:
         move.wait()
     total = 0
     for t in range(leaves):
-        for j in range(slots):
-            pair_t[total + j] = t
-            pair_s[total + j] = near_list[j, t] - window_start
-        total = total + near_count[t]
+        for j in range(1, slots):
+            pair_t[total + j - 1] = t
+            pair_s[total + j - 1] = near_list[j, t] - window_start
+        total = total + near_count[t] - 1
     for j in range(unroll + 1):
         pair_t[total + j] = leaves
         pair_s[total + j] = 0
     for ref, base, count in ((beside, beside_at, edge), (across, across_at, edge), (coords, edge, leaves)):
 
-        def put(row, value):
-            for q in range(points // 128):
-                feature_rows.at[q][pl.ds(16 * base + row, count, stride=16), :] = value[:, 128 * q : 128 * q + 128]
-
-        pieces(ref[0], ref[1], ref[2], put)
-
-    def rows_of(slot):
-        at = pl.ds(pl.multiple_of(16 * slot, 16), 16)
-        rows = jnp.concatenate([feature_rows[q, at, :].astype(bf16) for q in range(points // 128)], axis=1)
-        for b in range(4):
-            source_rows[slot, 16 * b : 16 * b + 16, :] = rows
-        return rows
+        spread(ref, base, count, feature_rows)
 
     def own(i, _):
-        target_rows[i] = targets_of(rows_of(edge + i), mix)
+        target_rows[i] = targets_of(source_of(edge + i, feature_rows, source_rows), mix)
         source_vals[edge + i] = rows8(charges[i])
         return 0
 
-    lax.fori_loop(0, leaves, own, 0, unroll=4)
+    lax.fori_loop(0, leaves, own, 0, unroll=own_unroll)
 
     def halo(g, _):
         for ref, base in ((beside, beside_at), (across, across_at)):
             for k in range(2):
-                rows_of(base + 2 * g + k)
+                source_of(base + 2 * g + k, feature_rows, source_rows)
                 source_vals[base + 2 * g + k] = rows8(ref[4 + g, 4 * k : 4 * k + 4, :])
         return 0
 
@@ -327,28 +416,29 @@
     trips = (total + unroll - 1) // unroll
     lax.fori_loop(0, trips, step, 0)
     for c in chunks:
-        apply(unroll * trips - 1, kern_b, c)
+        apply(jnp.maximum(unroll * trips - 1, 0), kern_b, c)
 
     def finish(i, _):
-        out[i] = fold8(total_rows[i])
+        out[i] = fold8(total_rows[i]) + self_part[i]
         return 0
 
     lax.fori_loop(0, leaves, finish, 0, unroll=4)
 
 
-def near_call(near_list, near_count, coords, charges, beside, across, chunk=128, unroll=4):
+def near_call(near_list, near_count, coords, charges, self_part, beside, across, chunk=128, unroll=4, own_unroll=4):
     leaves, _, points = charges.shape
     window = leaves + 2 * EDGE
     pairs = near_list.shape[0] * leaves + unroll + 4
     return pl.pallas_call(
-        functools.partial(near_body, chunk=chunk, unroll=unroll),
+        functools.partial(near_body, chunk=chunk, unroll=unroll, own_unroll=own_unroll),
         out_shape=jax.ShapeDtypeStruct((leaves, NRHS, points), f32),
-        in_specs=[HBM] * 4 + [VM] * 2,
+        in_specs=[HBM] * 5 + [VM] * 2,
         out_specs=VM,
         scratch_shapes=[
             pltpu.SMEM(near_list.shape, jnp.int32),
             pltpu.SMEM(near_count.shape, jnp.int32),
             pltpu.VMEM(coords.shape, f32),
+            pltpu.VMEM(charges.shape, f32),
             pltpu.VMEM(charges.shape, f32),
             pltpu.VMEM((leaves + 1, points, 64), bf16),
             pltpu.VMEM((window, 64, points), bf16),
@@ -361,11 +451,11 @@
             pltpu.VMEM((leaves + 1, 2 * NRHS, points), f32),
             pltpu.SMEM((pairs,), jnp.int32),
             pltpu.SMEM((pairs,), jnp.int32),
-            pltpu.SemaphoreType.DMA((4,)),
+            pltpu.SemaphoreType.DMA((5,)),
         ],
         compiler_params=pltpu.CompilerParams(vmem_limit_bytes=VMEM_LIMIT),
         name="near",
-    )(near_list, near_count, coords, charges, beside, across)
+    )(near_list, near_count, coords, charges, self_part, beside, across)
 
 
 def far_body(
@@ -378,8 +468,8 @@
     top_hbm,
     up_hbm,
     bases_hbm,
-    gathered,
-    near,
+    gathered_hbm,
+    near_hbm,
     out,
     far_mid,
     mid_count,
@@ -390,10 +480,13 @@
     top_transfer,
     up_transfer,
     bases,
+    gathered,
+    near,
     mid_points,
     top_points,
     pts,
     coef,
+    kern,
     sems,
 ):
     sources = (
@@ -403,11 +496,14 @@
         top_count_hbm,
         proxy_mid_hbm,
         proxy_top_hbm,
+        gathered_hbm,
         top_hbm,
         up_hbm,
         bases_hbm,
+        near_hbm,
     )
-    places = (far_mid, mid_count, far_top, top_count, proxy_mid, proxy_top, top_transfer, up_transfer, bases)
+    inputs = (far_mid, mid_count, far_top, top_count, proxy_mid, proxy_top)
+    places = inputs + (gathered, top_transfer, up_transfer, bases, near)
     moves = [pltpu.make_async_copy(src, dst, sems.at[k]) for k, (src, dst) in enumerate(zip(sources, places))]
     for move in moves:
         move.start()
@@ -417,6 +513,7 @@
     device = lax.axis_index("leaf")
     own = device * nodes
     parent = own // 8
+    mix = mixing()
     for move in moves[0:6]:
         move.wait()
     for k in range(3):
@@ -427,28 +524,42 @@
     def proxy(ref, node):
         return ref[pl.ds(4 * node, 3), :]
 
-    mix = mixing()
     lane = lax.broadcasted_iota(jnp.int32, (NRHS, 2 * rank), 1)
 
-    def field(node, ids, count, nodes_points, coeffs_of):
+    def kernels_of(k, node, ids, nodes_points):
         slots = ids.shape[0]
+        width = rank * slots
         for j in range(0, slots, 2):
             a, b = ids[j, node], ids[j + 1, node]
-            at = slice(rank * j, rank * j + 2 * rank)
-            pts[0:3, at] = jnp.where(lane[0:3] < rank, proxy(nodes_points, a), proxy(nodes_points, b))
-            left = jnp.where(j < count, coeffs_of(a, 0), 0.0)
-            right = jnp.where(j + 1 < count, coeffs_of(b, 1), 0.0)
-            coef[:, at] = jnp.where(lane < rank, left, right)
+            pts[k, 0:3, rank * j : rank * j + 2 * rank] = jnp.where(
+                lane[0:3] < rank, proxy(nodes_points, a), proxy(nodes_points, b)
+            )
+        rows = features(pts[k, 0:3, 0:width])
+        squared = jnp.dot(
+            targets_of(features(proxy(nodes_points, node)[:, 0:rank]), mix),
+            jnp.concatenate([rows] * 4, axis=0),
+            preferred_element_type=f32,
+        )
+        high, low = split2(covariance(squared))
+        kern[k, 0, :, 0:width] = high
+        kern[k, 1, :, 0:width] = low
+
+    def field(k, node, ids, count, coeffs_of):
+        slots = ids.shape[0]
         width = rank * slots
-        rows = features(pts[0:3, 0:width])
-        squared = jnp.dot(
-            targets_of(features(proxy(nodes_points, node)[:, 0:rank]), mix), jnp.concatenate([rows] * 4, axis=0), preferred_element_type=f32
+        for j in range(0, slots, 2):
+            left = jnp.where(j < count, coeffs_of(ids[j, node], 0), 0.0)
+            right = jnp.where(j + 1 < count, coeffs_of(ids[j + 1, node], 1), 0.0)
+            coef[k, :, rank * j : rank * j + 2 * rank] = jnp.where(lane < rank, left, right)
+        vals = rows8(coef[k, :, 0:width])
+        return fold8(
+            lax.dot_general(vals, kern[k, 0, :, 0:width], NT, preferred_element_type=f32)
+            + lax.dot_general(vals, kern[k, 1, :, 0:width], NT, preferred_element_type=f32)
         )
-        return fold8(dot2(rows8(coef[:, 0:width]), covariance(squared), NT))
 
     def mid_coeffs(s, half):
-        node = gathered[s // 2, 0:NRHS, :]
-        return jnp.where(s % 2 == half, node, pltpu.roll(node, rank, 1))
+        node = gathered[lax.shift_right_logical(s, 1), 0:NRHS, :]
+        return jnp.where((s & 1) == half, node, pltpu.roll(node, rank, 1))
 
     def top_coeffs(s, half):
         node = gathered[4 * s, NRHS : 2 * NRHS, :]
@@ -456,12 +567,14 @@
             node = node + gathered[4 * s + k, NRHS : 2 * NRHS, :]
         return node if half == 0 else pltpu.roll(node, rank, 1)
 
-    top_field = field(parent, far_top, top_count[parent], top_points, top_coeffs)
-    top8 = rows8(top_field)
+    kernels_of(nodes, parent, far_top, top_points)
+    for n in range(nodes):
+        kernels_of(n, own + n, far_mid, mid_points)
     for move in moves[6:]:
         move.wait()
+    top8 = rows8(field(nodes, parent, far_top, top_count[parent], top_coeffs))
     for n in range(nodes):
-        mid_field = field(own + n, far_mid, mid_count[own + n], mid_points, mid_coeffs)
+        mid_field = field(n, own + n, far_mid, mid_count[own + n], mid_coeffs)
         mid_field = mid_field + fold8(dot2(top8, top_transfer[n], (((1,), (0,)), ((), ()))))
         mid8 = rows8(mid_field)
         for leaf in range(8 * n, 8 * n + 8):
@@ -475,24 +588,26 @@
 ):
     width = bases.shape[1] * max(far_mid.shape[0], far_top.shape[0])
     integers = (far_mid, mid_count, far_top, top_count)
-    floats = (proxy_mid, proxy_top, top_transfer, up_transfer, bases)
+    floats = (proxy_mid, proxy_top, top_transfer, up_transfer, bases, gathered, near)
+    fields = near.shape[0] // 8 + 1
     return pl.pallas_call(
         far_body,
         out_shape=jax.ShapeDtypeStruct(near.shape, f32),
-        in_specs=[HBM] * 9 + [VM] * 2,
+        in_specs=[HBM] * 11,
         out_specs=VM,
         scratch_shapes=[pltpu.SMEM(a.shape, jnp.int32) for a in integers]
         + [pltpu.VMEM(a.shape, f32) for a in floats]
         + [
             pltpu.VMEM((4 * proxy_mid.shape[2], 2 * proxy_mid.shape[1]), f32),
             pltpu.VMEM((4 * proxy_top.shape[1], 2 * proxy_top.shape[2]), f32),
-            pltpu.VMEM((8, width), f32),
-            pltpu.VMEM((NRHS, width), f32),
-            pltpu.SemaphoreType.DMA((9,)),
+            pltpu.VMEM((fields, 8, width), f32),
+            pltpu.VMEM((fields, NRHS, width), f32),
+            pltpu.VMEM((fields, 2, bases.shape[1], width), bf16),
+            pltpu.SemaphoreType.DMA((11,)),
         ],
         compiler_params=pltpu.CompilerParams(vmem_limit_bytes=VMEM_LIMIT),
         name="far",
-    )(*integers, *floats, gathered, near)
+    )(*integers, *floats)
 
 
 def shards(
@@ -514,11 +629,11 @@
     chip = [(i, i ^ 1) for i in range(peers)]
     next_chip = [(i, i + 1 if i % 2 else i - 1) for i in range(1, peers - 1)]
     coords = jnp.transpose(coords, (1, 0, 2))
-    copies, beside, across = up_call(peers, coords, charges, bases, up_transfer, top_transfer)
+    copies, beside, across, self_part = up_call(peers, coords, charges, bases, up_transfer, top_transfer)
     across = lax.ppermute(across, "leaf", next_chip)
     beside = lax.ppermute(beside, "leaf", chip)
     gathered = lax.all_to_all(copies, "leaf", 0, 0, tiled=True)
-    near = near_call(near_list.T, near_count, coords, charges, beside, across)
+    near = near_call(near_list.T, near_count, coords, charges, self_part, beside, across)
     return far_call(
         far_mid.T,
         far_mid_count,

time: 67 us -> 66 us (0.985)
  local copies, waits for them, and re-layouts: 1.44 us -> 0 us
    pallas_call x2, Pallas kernels: 34.3 us -> 35.9 us  [the longest x1 20.3 us: near_call(): pl.pallas_call(functools.partial(near_body, chunk=chunk, unroll=unroll, o...]
    unnamed x6 -> x0, local copies, waits for them, and re-layouts: 1.44 us -> none
    pallas_call x1, Pallas kernels: 7.17 us -> 5.92 us  [far_call(): pl.pallas_call(far_body, out_shape=jax.ShapeDtypeStruct(near.shape, f32),...]
  transfers between devices with their start and end apart: 3 -> 3, of which waited for: 1 -> 1; matrix products, arithmetic and copies ran while one was open for 0% -> 0% of each run, Pallas kernels for 42% -> 31%
where the time goes in v4:
time: 66 us; the launch traced here: 65.7 us
  Pallas kernels  41.8 us (63%)
  starting transfers between devices  18.7 us (28%)
  waiting for transfers between devices  5.17 us (8%)
    pallas_call x1, Pallas kernels, near_call(): pl.pallas_call(functools.partial(near_body, chunk=chunk, unroll=unroll, o...  20.3 us
    pallas_call x1, Pallas kernels, up_call(): pl.pallas_call(functools.partial(up_body, self_unroll=self_unroll), out_s...  15.6 us
    all_to_all x1, starting transfers between devices, shards(): gathered = lax.all_to_all(copies, 'leaf', 0, 0, tiled=True)  11 us
    ppermute x1, starting transfers between devices, shards(): across = lax.ppermute(across, 'leaf', next_chip)  7.56 us
    pallas_call x1, Pallas kernels, far_call(): pl.pallas_call(far_body, out_shape=jax.ShapeDtypeStruct(near.shape, f32),...  5.92 us
    ppermute x1, waiting for transfers between devices, shards(): across = lax.ppermute(across, 'leaf', next_chip)  5.17 us
  transfers between devices with their start and end apart: 3, of which 1 were waited for; matrix products, arithmetic and copies ran while one was open for 0% of the time, Pallas kernels for 31%

profile of v4, /device:TPU:4, one launch (start us, length us, event | category | flops | bytes accessed | tf_op | source)
XLA Modules:
  0.0 65.7 jit_solution(14976969595692016306)
XLA Ops:
  0.0 15.6 %upward.1 = (f32[128,8,128]{2,1,0:T(8,128)}, f32[8,8,512]{2,1,0:T(8,128)}, f32[8,8,512]{2,1,0:T(8,128)}, f32[16,4,512]{2,1,0:T(4,128)}) custom-call(f32[3,16,512]{2,1,0:T(8,128)} %bitcast.6, f32[16,4,512]{2,1,0:T(4,128)} %charges_hbm.3, f32[16,64,512]{2,1,0:T(8,128)} %bases_hbm.3, f32[16,64,64]{2,1,0:T(8,128)} %up_hbm.3, f32[2,64,64]{2,1,0:T(8,128)} %top_hbm.3), custom_call_target="tpu_custom_call" | custom-call | tf_op jit(solution)/shard_map/upward/pallas_call | solution.py:282
  15.6 11.0 %all-to-all-start = ((f32[128,8,128]{2,1,0:T(8,128)}), f32[128,8,128]{2,1,0:T(8,128)}, u32[]{:S(2)}, u32[]{:S(2)}) async-start(f32[128,8,128]{2,1,0:T(8,128)} %get-tuple-element.9), calls=%async_computation | async-start | bytes 1048576 | tf_op jit(solution)/shard_map/all_to_all | solution.py:635
  26.6 0.2 collective-permute-start
  26.8 7.6 %collective-permute-start.1 = (f32[8,8,512]{2,1,0:T(8,128)}, f32[8,8,512]{2,1,0:T(8,128)}, u32[]{:S(2)}, u32[]{:S(2)}) collective-permute-start(f32[8,8,512]{2,1,0:T(8,128)} %get-tuple-element.12), channel_id=1, source_target_pairs={{1,2},{2,1},{3,4},{4,3},{5,6},{6,5},{7,8},{8,7},{9,10},{10,9},{11,... | collective-permute-start | bytes 393224 | tf_op jit(solution)/shard_map/ppermute | solution.py:633
  34.3 0.0 collective-permute-done.beside
  34.3 5.2 %collective-permute-done.1.across = f32[8,8,512]{2,1,0:T(8,128)} collective-permute-done((f32[8,8,512]{2,1,0:T(8,128)}, f32[8,8,512]{2,1,0:T(8,128)}, u32[]{:S(2)}, u32[]{:S(2)}) %collective-permute-start.1) | collective-permute-done | bytes 131104 | tf_op jit(solution)/shard_map/ppermute | solution.py:633
  39.5 20.3 %near.1.near_hbm = f32[16,4,512]{2,1,0:T(4,128)} custom-call(s32[4,16]{1,0:T(4,128)} %bitcast.12, s32[16]{0:T(128)} %count_hbm.1, f32[3,16,512]{2,1,0:T(8,128)} %bitcast.7, f32[16,4,512]{2,1,0:T(4,128)} %charges_hbm.3, f32[16,4,512]{2,1,0:T(4,128)} %get-tuple-element.10.self_hbm, f32[8,8,512]{2,1,0:T(8,128)} %collective-permute-done.beside, ...), custom_call_target="tpu_custom_call" | custom-call | tf_op jit(solution)/shard_map/near/pallas_call | solution.py:432
  59.8 0.0 all-to-all-done.gathered_hbm
  59.8 5.9 %far.1 = f32[16,4,512]{2,1,0:T(4,128)} custom-call(s32[32,256]{1,0:T(8,128)} %bitcast.10, s32[256]{0:T(256)} %mid_count_hbm.1, s32[6,32]{1,0:T(8,128)} %bitcast.11, s32[32]{0:T(128)} %top_count_hbm.1, f32[3,64,256]{2,1,0:T(8,128)} %bitcast.8, f32[3,32,64]{2,1,0:T(8,128)} %bitcast.9, f32[2,64,64]{2,1,0:T(8,128)} %top_hbm.3, f32[16,64,64]{2,1,0:T(8,128)} %up_hbm.3, ...), custom_call_target="tpu_custom_call" | custom-call | tf_op jit(solution)/shard_map/far/pallas_call | solution.py:593
Async XLA Ops:
  15.6 44.2 %all-to-all-start = ((f32[128,8,128]{2,1,0:T(8,128)}), f32[128,8,128]{2,1,0:T(8,128)}, u32[]{:S(2)}, u32[]{:S(2)}) async-start(f32[128,8,128]{2,1,0:T(8,128)} %get-tuple-element.9), calls=%async_computation | async-start | bytes 1048576 | tf_op jit(solution)/shard_map/all_to_all | solution.py:635
  26.6 7.8 %collective-permute-start = (f32[8,8,512]{2,1,0:T(8,128)}, f32[8,8,512]{2,1,0:T(8,128)}, u32[]{:S(2)}, u32[]{:S(2)}) collective-permute-start(f32[8,8,512]{2,1,0:T(8,128)} %get-tuple-element.11), channel_id=1, source_target_pairs={{0,1},{1,0},{2,3},{3,2},{4,5},{5,4},{6,7},{7,6},{8,9},{9,8},{10,11... | collective-permute-start | bytes 393224 | tf_op jit(solution)/shard_map/ppermute | solution.py:634
  26.8 12.7 %collective-permute-start.1 = (f32[8,8,512]{2,1,0:T(8,128)}, f32[8,8,512]{2,1,0:T(8,128)}, u32[]{:S(2)}, u32[]{:S(2)}) collective-permute-start(f32[8,8,512]{2,1,0:T(8,128)} %get-tuple-element.12), channel_id=1, source_target_pairs={{1,2},{2,1},{3,4},{4,3},{5,6},{6,5},{7,8},{8,7},{9,10},{10,9},{11,... | collective-permute-start | bytes 393224 | tf_op jit(solution)/shard_map/ppermute | solution.py:633

commit v5 on v4

--- a/solution.py
+++ b/solution.py
@@ -16,6 +16,7 @@
 RATE = -1.4426950408889634 / length_scale
 NT = (((1,), (1,)), ((), ()))
 TN = (((0,), (0,)), ((), ()))
+NN = (((1,), (0,)), ((), ()))
 bf16 = jnp.bfloat16
 f32 = jnp.float32
 VM = pl.BlockSpec(memory_space=pltpu.VMEM)
@@ -200,7 +201,7 @@
         source_vals[i] = rows8(charges[i])
         return 0
 
-    lax.fori_loop(0, leaves, own, 0, unroll=4)
+    lax.fori_loop(0, leaves, own, 0, unroll=16)
 
     def self_distances(t, dst, c):
         rows = slice(c, c + BLOCK)
@@ -248,21 +249,20 @@
         self_part[leaf] = fold8(total_rows[leaf])
     sends.append(pltpu.make_async_copy(self_part, self_hbm, sems.at[6]))
     sends[2].start()
+    for pair in moves:
+        for move in pair:
+            move.wait()
+    small[2].wait()
+    coeffs = [rows8(fold8(dot2(source_vals[leaf], bases[leaf], NT))) for leaf in range(leaves)]
+    parts = [fold8(dot2(coeffs[leaf], up_transfer[leaf], NT)) for leaf in range(leaves)]
     mids = []
     lift = None
     for n in range(leaves // 8):
-        mid = None
-        for g in range(2 * n, 2 * n + 2):
-            for move in moves[g]:
-                move.wait()
-            for leaf in range(group * g, group * g + group):
-                coeffs = fold8(dot2(rows8(charges[leaf]), bases[leaf], NT))
-                part = fold8(dot2(rows8(coeffs), up_transfer[leaf], NT))
-                mid = part if mid is None else mid + part
-        mids.append(mid)
-        if n == 0:
-            small[2].wait()
-        part = fold8(dot2(rows8(mid), top_transfer[n], NT))
+        group = parts[8 * n : 8 * n + 8]
+        while len(group) > 1:
+            group = [a + b for a, b in zip(group[0::2], group[1::2])]
+        mids.append(group[0])
+        part = fold8(dot2(rows8(group[0]), top_transfer[n], NT))
         lift = part if lift is None else lift + part
     tile = jnp.concatenate(
         [jnp.concatenate(mids, axis=1), jnp.concatenate([lift, jnp.zeros_like(lift)], axis=1)], axis=0
@@ -425,7 +425,7 @@
     lax.fori_loop(0, leaves, finish, 0, unroll=4)
 
 
-def near_call(near_list, near_count, coords, charges, self_part, beside, across, chunk=128, unroll=4, own_unroll=4):
+def near_call(near_list, near_count, coords, charges, self_part, beside, across, chunk=128, unroll=4, own_unroll=16):
     leaves, _, points = charges.shape
     window = leaves + 2 * EDGE
     pairs = near_list.shape[0] * leaves + unroll + 4
@@ -573,14 +573,15 @@
     for move in moves[6:]:
         move.wait()
     top8 = rows8(field(nodes, parent, far_top, top_count[parent], top_coeffs))
+    mids = []
     for n in range(nodes):
         mid_field = field(n, own + n, far_mid, mid_count[own + n], mid_coeffs)
         mid_field = mid_field + fold8(dot2(top8, top_transfer[n], (((1,), (0,)), ((), ()))))
         mid8 = rows8(mid_field)
-        for leaf in range(8 * n, 8 * n + 8):
-            leaf_field = fold8(dot2(mid8, up_transfer[leaf], (((1,), (0,)), ((), ()))))
-            far = fold8(dot2(rows8(leaf_field), bases[leaf], (((1,), (0,)), ((), ()))))
-            out[leaf] = (near[leaf] + far) * out_scale
+        mids.append(mid8)
+    fields = [rows8(fold8(dot2(mids[leaf // 8], up_transfer[leaf], NN))) for leaf in range(leaves)]
+    for leaf in range(leaves):
+        out[leaf] = (near[leaf] + fold8(dot2(fields[leaf], bases[leaf], NN))) * out_scale
 
 
 def far_call(

time: 66 us -> 60.1 us (0.911)
  Pallas kernels: 41.8 us -> 35.9 us
    pallas_call x1, Pallas kernels: 15.6 us -> 12 us  [up_call(): pl.pallas_call(functools.partial(up_body, self_unroll=self_unroll), out_s...]
    pallas_call x1, Pallas kernels: 5.92 us -> 4.33 us  [far_call(): pl.pallas_call(far_body, out_shape=jax.ShapeDtypeStruct(near.shape, f32),...]
    pallas_call x1, Pallas kernels: 20.3 us -> 19.6 us  [near_call(): pl.pallas_call(functools.partial(near_body, chunk=chunk, unroll=unroll, o...]
  transfers between devices with their start and end apart: 3 -> 3, of which waited for: 1 -> 1; matrix products, arithmetic and copies ran while one was open for 0% -> 0% of each run, Pallas kernels for 31% -> 33%
where the time goes in v5:
time: 60.1 us; the launch traced here: 59.9 us
  Pallas kernels  35.9 us (60%)
  starting transfers between devices  18.7 us (31%)
  waiting for transfers between devices  5.17 us (9%)
    pallas_call x1, Pallas kernels, near_call(): pl.pallas_call(functools.partial(near_body, chunk=chunk, unroll=unroll, o...  19.6 us
    pallas_call x1, Pallas kernels, up_call(): pl.pallas_call(functools.partial(up_body, self_unroll=self_unroll), out_s...  12 us
    all_to_all x1, starting transfers between devices, shards(): gathered = lax.all_to_all(copies, 'leaf', 0, 0, tiled=True)  11 us
    ppermute x1, starting transfers between devices, shards(): across = lax.ppermute(across, 'leaf', next_chip)  7.56 us
    ppermute x1, waiting for transfers between devices, shards(): across = lax.ppermute(across, 'leaf', next_chip)  5.17 us
    pallas_call x1, Pallas kernels, far_call(): pl.pallas_call(far_body, out_shape=jax.ShapeDtypeStruct(near.shape, f32),...  4.33 us
  transfers between devices with their start and end apart: 3, of which 1 were waited for; matrix products, arithmetic and copies ran while one was open for 0% of the time, Pallas kernels for 33%

profile of v5, /device:TPU:4, one launch (start us, length us, event | category | flops | bytes accessed | tf_op | source)
XLA Modules:
  0.0 59.9 jit_solution(2789038395726989161)
XLA Ops:
  0.0 12.0 %upward.1 = (f32[128,8,128]{2,1,0:T(8,128)}, f32[8,8,512]{2,1,0:T(8,128)}, f32[8,8,512]{2,1,0:T(8,128)}, f32[16,4,512]{2,1,0:T(4,128)}) custom-call(f32[3,16,512]{2,1,0:T(8,128)} %bitcast.6, f32[16,4,512]{2,1,0:T(4,128)} %charges_hbm.3, f32[16,64,512]{2,1,0:T(8,128)} %bases_hbm.3, f32[16,64,64]{2,1,0:T(8,128)} %up_hbm.3, f32[2,64,64]{2,1,0:T(8,128)} %top_hbm.3), custom_call_target="tpu_custom_call" | custom-call | tf_op jit(solution)/shard_map/upward/pallas_call | solution.py:282
  12.1 11.0 %all-to-all-start = ((f32[128,8,128]{2,1,0:T(8,128)}), f32[128,8,128]{2,1,0:T(8,128)}, u32[]{:S(2)}, u32[]{:S(2)}) async-start(f32[128,8,128]{2,1,0:T(8,128)} %get-tuple-element.9), calls=%async_computation | async-start | bytes 1048576 | tf_op jit(solution)/shard_map/all_to_all | solution.py:636
  23.0 0.2 collective-permute-start
  23.2 7.6 %collective-permute-start.1 = (f32[8,8,512]{2,1,0:T(8,128)}, f32[8,8,512]{2,1,0:T(8,128)}, u32[]{:S(2)}, u32[]{:S(2)}) collective-permute-start(f32[8,8,512]{2,1,0:T(8,128)} %get-tuple-element.12), channel_id=1, source_target_pairs={{1,2},{2,1},{3,4},{4,3},{5,6},{6,5},{7,8},{8,7},{9,10},{10,9},{11,... | collective-permute-start | bytes 393224 | tf_op jit(solution)/shard_map/ppermute | solution.py:634
  30.8 0.0 collective-permute-done.beside
  30.8 5.2 %collective-permute-done.1.across = f32[8,8,512]{2,1,0:T(8,128)} collective-permute-done((f32[8,8,512]{2,1,0:T(8,128)}, f32[8,8,512]{2,1,0:T(8,128)}, u32[]{:S(2)}, u32[]{:S(2)}) %collective-permute-start.1) | collective-permute-done | bytes 131104 | tf_op jit(solution)/shard_map/ppermute | solution.py:634
  36.0 19.6 %near.1.near_hbm = f32[16,4,512]{2,1,0:T(4,128)} custom-call(s32[4,16]{1,0:T(4,128)} %bitcast.12, s32[16]{0:T(128)} %count_hbm.1, f32[3,16,512]{2,1,0:T(8,128)} %bitcast.7, f32[16,4,512]{2,1,0:T(4,128)} %charges_hbm.3, f32[16,4,512]{2,1,0:T(4,128)} %get-tuple-element.10.self_hbm, f32[8,8,512]{2,1,0:T(8,128)} %collective-permute-done.beside, ...), custom_call_target="tpu_custom_call" | custom-call | tf_op jit(solution)/shard_map/near/pallas_call | solution.py:432
  55.5 0.0 all-to-all-done.gathered_hbm
  55.5 4.3 %far.1 = f32[16,4,512]{2,1,0:T(4,128)} custom-call(s32[32,256]{1,0:T(8,128)} %bitcast.10, s32[256]{0:T(256)} %mid_count_hbm.1, s32[6,32]{1,0:T(8,128)} %bitcast.11, s32[32]{0:T(128)} %top_count_hbm.1, f32[3,64,256]{2,1,0:T(8,128)} %bitcast.8, f32[3,32,64]{2,1,0:T(8,128)} %bitcast.9, f32[2,64,64]{2,1,0:T(8,128)} %top_hbm.3, f32[16,64,64]{2,1,0:T(8,128)} %up_hbm.3, ...), custom_call_target="tpu_custom_call" | custom-call | tf_op jit(solution)/shard_map/far/pallas_call | solution.py:594
Async XLA Ops:
  12.1 43.5 %all-to-all-start = ((f32[128,8,128]{2,1,0:T(8,128)}), f32[128,8,128]{2,1,0:T(8,128)}, u32[]{:S(2)}, u32[]{:S(2)}) async-start(f32[128,8,128]{2,1,0:T(8,128)} %get-tuple-element.9), calls=%async_computation | async-start | bytes 1048576 | tf_op jit(solution)/shard_map/all_to_all | solution.py:636
  23.0 7.8 %collective-permute-start = (f32[8,8,512]{2,1,0:T(8,128)}, f32[8,8,512]{2,1,0:T(8,128)}, u32[]{:S(2)}, u32[]{:S(2)}) collective-permute-start(f32[8,8,512]{2,1,0:T(8,128)} %get-tuple-element.11), channel_id=1, source_target_pairs={{0,1},{1,0},{2,3},{3,2},{4,5},{5,4},{6,7},{7,6},{8,9},{9,8},{10,11... | collective-permute-start | bytes 393224 | tf_op jit(solution)/shard_map/ppermute | solution.py:635
  23.2 12.7 %collective-permute-start.1 = (f32[8,8,512]{2,1,0:T(8,128)}, f32[8,8,512]{2,1,0:T(8,128)}, u32[]{:S(2)}, u32[]{:S(2)}) collective-permute-start(f32[8,8,512]{2,1,0:T(8,128)} %get-tuple-element.12), channel_id=1, source_target_pairs={{1,2},{2,1},{3,4},{4,3},{5,6},{6,5},{7,8},{8,7},{9,10},{10,9},{11,... | collective-permute-start | bytes 393224 | tf_op jit(solution)/shard_map/ppermute | solution.py:634

commit v6 on v5

--- a/solution.py
+++ b/solution.py
@@ -570,16 +570,15 @@
     kernels_of(nodes, parent, far_top, top_points)
     for n in range(nodes):
         kernels_of(n, own + n, far_mid, mid_points)
-    for move in moves[6:]:
-        move.wait()
+    moves[6].wait()
     top8 = rows8(field(nodes, parent, far_top, top_count[parent], top_coeffs))
-    mids = []
-    for n in range(nodes):
-        mid_field = field(n, own + n, far_mid, mid_count[own + n], mid_coeffs)
-        mid_field = mid_field + fold8(dot2(top8, top_transfer[n], (((1,), (0,)), ((), ()))))
-        mid8 = rows8(mid_field)
-        mids.append(mid8)
+    sums = [field(n, own + n, far_mid, mid_count[own + n], mid_coeffs) for n in range(nodes)]
+    moves[7].wait()
+    moves[8].wait()
+    mids = [rows8(sums[n] + fold8(dot2(top8, top_transfer[n], NN))) for n in range(nodes)]
     fields = [rows8(fold8(dot2(mids[leaf // 8], up_transfer[leaf], NN))) for leaf in range(leaves)]
+    moves[9].wait()
+    moves[10].wait()
     for leaf in range(leaves):
         out[leaf] = (near[leaf] + fold8(dot2(fields[leaf], bases[leaf], NN))) * out_scale
 

time: 60.1 us -> 60.4 us (level)
  no operation moved by 1% of the time
where the time goes in v6:
time: 60.4 us; the launch traced here: 60.1 us
  Pallas kernels  36.2 us (60%)
  starting transfers between devices  18.7 us (31%)
  waiting for transfers between devices  5.17 us (9%)
    pallas_call x1, Pallas kernels, near_call(): pl.pallas_call(functools.partial(near_body, chunk=chunk, unroll=unroll, o...  19.6 us
    pallas_call x1, Pallas kernels, up_call(): pl.pallas_call(functools.partial(up_body, self_unroll=self_unroll), out_s...  12 us
    all_to_all x1, starting transfers between devices, shards(): gathered = lax.all_to_all(copies, 'leaf', 0, 0, tiled=True)  11 us
    ppermute x1, starting transfers between devices, shards(): across = lax.ppermute(across, 'leaf', next_chip)  7.56 us
    ppermute x1, waiting for transfers between devices, shards(): across = lax.ppermute(across, 'leaf', next_chip)  5.17 us
    pallas_call x1, Pallas kernels, far_call(): pl.pallas_call(far_body, out_shape=jax.ShapeDtypeStruct(near.shape, f32),...  4.61 us
  transfers between devices with their start and end apart: 3, of which 1 were waited for; matrix products, arithmetic and copies ran while one was open for 0% of the time, Pallas kernels for 33%

profile of v6, /device:TPU:4, one launch (start us, length us, event | category | flops | bytes accessed | tf_op | source)
XLA Modules:
  0.0 60.1 jit_solution(5440306970216513178)
XLA Ops:
  0.0 12.0 %upward.1 = (f32[128,8,128]{2,1,0:T(8,128)}, f32[8,8,512]{2,1,0:T(8,128)}, f32[8,8,512]{2,1,0:T(8,128)}, f32[16,4,512]{2,1,0:T(4,128)}) custom-call(f32[3,16,512]{2,1,0:T(8,128)} %bitcast.6, f32[16,4,512]{2,1,0:T(4,128)} %charges_hbm.3, f32[16,64,512]{2,1,0:T(8,128)} %bases_hbm.3, f32[16,64,64]{2,1,0:T(8,128)} %up_hbm.3, f32[2,64,64]{2,1,0:T(8,128)} %top_hbm.3), custom_call_target="tpu_custom_call" | custom-call | tf_op jit(solution)/shard_map/upward/pallas_call | solution.py:282
  12.1 11.0 %all-to-all-start = ((f32[128,8,128]{2,1,0:T(8,128)}), f32[128,8,128]{2,1,0:T(8,128)}, u32[]{:S(2)}, u32[]{:S(2)}) async-start(f32[128,8,128]{2,1,0:T(8,128)} %get-tuple-element.9), calls=%async_computation | async-start | bytes 1048576 | tf_op jit(solution)/shard_map/all_to_all | solution.py:635
  23.0 0.2 collective-permute-start
  23.2 7.6 %collective-permute-start.1 = (f32[8,8,512]{2,1,0:T(8,128)}, f32[8,8,512]{2,1,0:T(8,128)}, u32[]{:S(2)}, u32[]{:S(2)}) collective-permute-start(f32[8,8,512]{2,1,0:T(8,128)} %get-tuple-element.12), channel_id=1, source_target_pairs={{1,2},{2,1},{3,4},{4,3},{5,6},{6,5},{7,8},{8,7},{9,10},{10,9},{11,... | collective-permute-start | bytes 393224 | tf_op jit(solution)/shard_map/ppermute | solution.py:633
  30.8 0.0 collective-permute-done.beside
  30.8 5.2 %collective-permute-done.1.across = f32[8,8,512]{2,1,0:T(8,128)} collective-permute-done((f32[8,8,512]{2,1,0:T(8,128)}, f32[8,8,512]{2,1,0:T(8,128)}, u32[]{:S(2)}, u32[]{:S(2)}) %collective-permute-start.1) | collective-permute-done | bytes 131104 | tf_op jit(solution)/shard_map/ppermute | solution.py:633
  36.0 19.6 %near.1.near_hbm = f32[16,4,512]{2,1,0:T(4,128)} custom-call(s32[4,16]{1,0:T(4,128)} %bitcast.12, s32[16]{0:T(128)} %count_hbm.1, f32[3,16,512]{2,1,0:T(8,128)} %bitcast.7, f32[16,4,512]{2,1,0:T(4,128)} %charges_hbm.3, f32[16,4,512]{2,1,0:T(4,128)} %get-tuple-element.10.self_hbm, f32[8,8,512]{2,1,0:T(8,128)} %collective-permute-done.beside, ...), custom_call_target="tpu_custom_call" | custom-call | tf_op jit(solution)/shard_map/near/pallas_call | solution.py:432
  55.5 0.0 all-to-all-done.gathered_hbm
  55.5 4.6 %far.1 = f32[16,4,512]{2,1,0:T(4,128)} custom-call(s32[32,256]{1,0:T(8,128)} %bitcast.10, s32[256]{0:T(256)} %mid_count_hbm.1, s32[6,32]{1,0:T(8,128)} %bitcast.11, s32[32]{0:T(128)} %top_count_hbm.1, f32[3,64,256]{2,1,0:T(8,128)} %bitcast.8, f32[3,32,64]{2,1,0:T(8,128)} %bitcast.9, f32[2,64,64]{2,1,0:T(8,128)} %top_hbm.3, f32[16,64,64]{2,1,0:T(8,128)} %up_hbm.3, ...), custom_call_target="tpu_custom_call" | custom-call | tf_op jit(solution)/shard_map/far/pallas_call | solution.py:593
Async XLA Ops:
  12.1 43.5 %all-to-all-start = ((f32[128,8,128]{2,1,0:T(8,128)}), f32[128,8,128]{2,1,0:T(8,128)}, u32[]{:S(2)}, u32[]{:S(2)}) async-start(f32[128,8,128]{2,1,0:T(8,128)} %get-tuple-element.9), calls=%async_computation | async-start | bytes 1048576 | tf_op jit(solution)/shard_map/all_to_all | solution.py:635
  23.0 7.8 %collective-permute-start = (f32[8,8,512]{2,1,0:T(8,128)}, f32[8,8,512]{2,1,0:T(8,128)}, u32[]{:S(2)}, u32[]{:S(2)}) collective-permute-start(f32[8,8,512]{2,1,0:T(8,128)} %get-tuple-element.11), channel_id=1, source_target_pairs={{0,1},{1,0},{2,3},{3,2},{4,5},{5,4},{6,7},{7,6},{8,9},{9,8},{10,11... | collective-permute-start | bytes 393224 | tf_op jit(solution)/shard_map/ppermute | solution.py:634
  23.2 12.7 %collective-permute-start.1 = (f32[8,8,512]{2,1,0:T(8,128)}, f32[8,8,512]{2,1,0:T(8,128)}, u32[]{:S(2)}, u32[]{:S(2)}) collective-permute-start(f32[8,8,512]{2,1,0:T(8,128)} %get-tuple-element.12), channel_id=1, source_target_pairs={{1,2},{2,1},{3,4},{4,3},{5,6},{6,5},{7,8},{8,7},{9,10},{10,9},{11,... | collective-permute-start | bytes 393224 | tf_op jit(solution)/shard_map/ppermute | solution.py:633
